TPU v7x, 32 devices: a whole 2x2x4 slice. The times are simulated.
32 devices in a mesh: freq: 2 (over y), rcv: 4 (over z), src: 4 (over x, core).
Axes of the slice: x: 2, y: 2, z: 4, core: 2. Of those that a mesh axis runs over, the one named last changes fastest.
Arguments:
- traces: float32 [256, 2, 4096], P(('freq', 'src'), None, 'rcv'), parts along dimension 0, may hold values from -6 to 6
- moveout: float32 [2, 64, 16], P(None, 'freq'), parts along dimension 1, may hold values from -0.75 to 0.75
- trace_owner: int32 [8192], P(('freq', 'rcv')), parts along dimension 0, may hold values from 0 to 3, as said below
- trace_group: int32 [8192], P(('freq', 'rcv')), parts along dimension 0, may hold values from 0 to 127
- trace_table: int32 [8192], P(('freq', 'rcv')), parts along dimension 0, may hold values from 0 to 31
- aperture: float32 [2, 16384, 8192], P(None, ('freq', 'rcv'), 'src'), parts along dimension 1, may hold values from -0.046875 to 0.046875
- shaping: float32 [256, 2, 8192], P(('freq', 'src'), None, 'rcv'), parts along dimension 0, may hold values from -0.5 to 0.5
Outputs:
- demultiple: float32 [256, 2, 8192], P(('freq', 'src'), None, 'rcv'), parts along dimension 0
There are 2 independent parts, one for each index of `freq`. A program takes and returns all parts, laid end to end along the dimension named above; each array names one. Nothing has to cross between parts.
Inputs may be any that keep to these rules, and one draw needn't show every extreme that they name: `trace_owner`: among the 1024 traces of each index of rcv (aligned blocks of the array), at most 512 name the same owner, and in every draw some owner is named by exactly 512 traces of every block.
All inputs are finite; a program needn't handle non-finite values.
Results may differ from a plain program's by a relative error of at most 0.0001.
Values sent between devices are 32-bit elements; how exact they have to be, the bound alone decides.
A program may use at most 128 MiB of HBM per device.

v0:
```python
import functools

import jax
import jax.numpy as jnp
from jax import lax
from jax.experimental import pallas as pl
from jax.experimental.pallas import tpu as pltpu
from jax.sharding import PartitionSpec as P

ITERS = 2
MESH = pl.DeviceIdType.MESH
F32 = jnp.float32
BF16 = jnp.bfloat16
NT = (((1,), (1,)), ((), ()))


def split(value):
    high = value.astype(BF16)
    return high, (value - high.astype(F32)).astype(BF16)


def remote(src, dst, send_sem, recv_sem, where):
    return pltpu.make_async_remote_copy(
        src_ref=src,
        dst_ref=dst,
        send_sem=send_sem,
        recv_sem=recv_sem,
        device_id=where,
        device_id_type=MESH,
    )


def pieces(refs_shape, count):
    planes, rows = refs_shape[0], refs_shape[1]
    per = max(1, count // planes)
    step = rows // per
    return [(p, pl.ds(h * step, step)) for p in range(planes) for h in range(per)]


def gather_kernel(nz, ns, fold, plane, cuts, in_ref, out_ref, *scratch):
    if plane:
        held, zs, zr, ps, pr, ls = scratch
    else:
        held = out_ref
        zs, zr, ls = scratch
    z = lax.axis_index("rcv")
    c = lax.axis_index("src")
    width = in_ref.shape[-1]
    rows = in_ref.shape[1]

    barrier = pltpu.get_barrier_semaphore()
    for way in (1, -1):
        near = z + way

        @pl.when((near >= 0) & (near < nz))
        def _():
            pl.semaphore_signal(barrier, inc=1, device_id={"rcv": near}, device_id_type=MESH)

    if plane:
        for off in range(1, ns):
            pl.semaphore_signal(
                barrier, inc=1, device_id={"src": lax.rem(c + off, ns)}, device_id_type=MESH
            )
    peers = jnp.where(z > 0, 1, 0) + jnp.where(z < nz - 1, 1, 0)
    pl.semaphore_wait(barrier, peers + (ns - 1 if plane else 0))

    def along(src, block, lane, dist, q):
        way = 1 - 2 * lane
        cut = cuts[q]
        return remote(
            src.at[cut] if src is in_ref else src.at[(block,) + cut],
            held.at[(block,) + cut],
            zs.at[lane, dist, q],
            zr.at[lane, dist, q],
            {"rcv": z + way},
        )

    def place(who, f, q):
        p, r = cuts[q]
        return out_ref.at[
            p, pl.ds(pl.multiple_of(who * rows + r.start, 8), r.size), pl.ds(f * width, width)
        ]

    def across(src, block, q):
        f = block - (block // fold) * fold
        cut = cuts[q]
        return remote(
            src.at[cut] if src is in_ref else src.at[(block,) + cut],
            place(c, f, q),
            ps.at[block, q],
            pr.at[c, f, q],
            {"src": block // fold},
        )

    def local(src, block, q):
        f = block - (block // fold) * fold if plane else 0
        cut = cuts[q]
        there = place(c, f, q) if plane else held.at[(block,) + cut]
        here = src.at[cut] if src is in_ref else src.at[(block,) + cut]
        return pltpu.make_async_copy(here, there, ls.at[f, q])

    def hand_on(src, block, q):
        if not plane:
            return

        @pl.when(block // fold != c)
        def _():
            across(src, block, q).start()

        @pl.when(block // fold == c)
        def _():
            local(src, block, q).start()

    def has(lane):
        near = z + 1 - 2 * lane
        return (near >= 0) & (near < nz)

    for q in range(len(cuts)):
        for lane in (0, 1):

            @pl.when(has(lane))
            def _():
                along(in_ref, z, lane, 0, q).start()

        if plane:
            hand_on(in_ref, z, q)
        else:
            local(in_ref, z, q).start()

    def hop(dist, carry):
        for q in range(len(cuts)):
            for lane in (0, 1):
                block = z - dist * (1 - 2 * lane)

                @pl.when((block >= 0) & (block < nz))
                def _():
                    along(held, block, lane, dist - 1, q).wait_recv()

                    @pl.when(has(lane))
                    def _():
                        along(held, block, lane, dist, q).start()

                    hand_on(held, block, q)

        return carry

    lax.fori_loop(1, nz, hop, 0)

    def drain(dist, carry):
        for q in range(len(cuts)):
            for lane in (0, 1):
                block = z - dist * (1 - 2 * lane)

                @pl.when((block >= 0) & (block < nz) & has(lane))
                def _():
                    along(held, block, lane, dist, q).wait_send()

            if plane:

                @pl.when(dist // fold != c)
                def _():
                    across(held, dist, q).wait_send()

                @pl.when(dist // fold == c)
                def _():
                    local(held, dist, q).wait()

        return carry

    lax.fori_loop(0, nz, drain, 0)
    for q in range(len(cuts)):
        if not plane:
            local(in_ref, z, q).wait()
        else:
            for off in range(1, ns):
                who = lax.rem(c + off, ns)
                for f in range(fold):
                    remote(
                        place(who, f, q),
                        place(who, f, q),
                        ps.at[0, q],
                        pr.at[who, f, q],
                        {"src": who},
                    ).wait_recv()


def gather(value, nz, ns, plane, count, cid, name):
    planes, rows, width = value.shape
    fold = nz // ns
    cuts = pieces(value.shape, count)
    nq = len(cuts)
    dma = pltpu.SemaphoreType.DMA
    scratch = [dma((2, nz, nq)), dma((2, nz, nq))]
    if plane:
        out = jax.ShapeDtypeStruct((planes, ns * rows, fold * width), F32)
        scratch = [pltpu.VMEM((nz,) + value.shape, F32)] + scratch
        scratch += [dma((nz, nq)), dma((ns, fold, nq)), dma((fold, nq))]
    else:
        out = jax.ShapeDtypeStruct((nz,) + value.shape, F32)
        scratch += [dma((1, nq))]
    return pl.pallas_call(
        functools.partial(gather_kernel, nz, ns, fold, plane, cuts),
        out_shape=out,
        in_specs=[pl.BlockSpec(memory_space=pltpu.VMEM)],
        out_specs=pl.BlockSpec(memory_space=pltpu.VMEM),
        scratch_shapes=scratch,
        name=name,
        compiler_params=pltpu.CompilerParams(collective_id=cid, has_side_effects=True),
    )(value)


def bin_kernel(
    nz, cuts, groups, tables, shots, in_ref, wt_ref, out_ref, held, terms, total, order, zs, zr
):
    z = lax.axis_index("rcv")
    stencil = wt_ref.shape[0] // 2
    rows = 2 * shots
    width = in_ref.shape[-1]
    cells = nz * groups

    def has(lane):
        near = z + 1 - 2 * lane
        return (near >= 0) & (near < nz)

    barrier = pltpu.get_barrier_semaphore()
    for lane in (0, 1):

        @pl.when(has(lane))
        def _():
            pl.semaphore_signal(
                barrier, inc=1, device_id={"rcv": z + 1 - 2 * lane}, device_id_type=MESH
            )

    pl.semaphore_wait(barrier, jnp.where(z > 0, 1, 0) + jnp.where(z < nz - 1, 1, 0))

    def along(own, block, lane, dist, q):
        cut = cuts[q]
        return remote(
            in_ref.at[cut] if own else held.at[(block,) + cut],
            held.at[(block,) + cut],
            zs.at[lane, dist, q],
            zr.at[lane, dist, q],
            {"rcv": z + 1 - 2 * lane},
        )

    for q in range(len(cuts)):
        for lane in (0, 1):

            @pl.when(has(lane))
            def _():
                along(True, z, lane, 0, q).start()

    w = wt_ref[...]
    w0 = w.astype(BF16)
    rest = w - w0.astype(F32)
    w1 = rest.astype(BF16)
    w2 = (rest - w1.astype(F32)).astype(BF16)
    table_ids = lax.broadcasted_iota(jnp.int32, (tables, width), 0).astype(F32)
    cell_ids = lax.broadcasted_iota(jnp.int32, (cells, width), 0).astype(F32)

    def sums(view):
        cell = view[0, rows : rows + 1, :] * float(groups) + view[0, rows + 1 : rows + 2, :]
        table_hot = (table_ids == view[0, rows + 2 : rows + 3, :]).astype(BF16)
        picked = sum(
            jnp.dot(part, table_hot, preferred_element_type=F32) for part in (w0, w1, w2)
        )
        hot = (cell_ids == cell).astype(BF16)
        real = view[0, 0:shots, :]
        imag = view[0, shots:rows, :]
        for j in range(stencil):
            wr = picked[j : j + 1, :]
            wi = picked[stencil + j : stencil + j + 1, :]
            base = j * 2 * rows
            for part, both in enumerate((real * wr - imag * wi, real * wi + imag * wr)):
                high, low = split(both)
                at = base + part * shots
                terms[at : at + shots, :] = high
                terms[at + rows : at + rows + shots, :] = low
        found = lax.dot_general(terms[...], hot, NT, preferred_element_type=F32)
        found = found.reshape(stencil, 2, rows, cells)
        return found[:, 0] + found[:, 1]

    total[...] = sums(in_ref)

    def hop(dist, carry):
        for q in range(len(cuts)):
            for lane in (0, 1):
                block = z - dist * (1 - 2 * lane)

                @pl.when((block >= 0) & (block < nz))
                def _():
                    along(False, block, lane, dist - 1, q).wait_recv()

                    @pl.when(has(lane))
                    def _():
                        along(False, block, lane, dist, q).start()

        def add(lane, inner):
            block = z - dist * (1 - 2 * lane)

            @pl.when((block >= 0) & (block < nz))
            def _():
                total[...] += sums(held.at[block])

            return inner

        return lax.fori_loop(0, 2, add, carry)

    lax.fori_loop(1, nz, hop, 0)
    for j in range(stencil):
        order[:, j, :] = total[j].T
    out_ref[...] = order[...].reshape(cells * stencil, rows).T

    def drain(dist, carry):
        for q in range(len(cuts)):
            for lane in (0, 1):
                block = z - dist * (1 - 2 * lane)

                @pl.when((block >= 0) & (block < nz) & has(lane))
                def _():
                    along(False, block, lane, dist, q).wait_send()

        return carry

    lax.fori_loop(0, nz, drain, 0)


def bin_all(value, moveout, nz, groups, shots, cid):
    tables, stencil = moveout.shape[1:]
    width = value.shape[-1]
    weights = jnp.transpose(moveout, (0, 2, 1)).reshape(2 * stencil, tables)
    cuts = pieces(value.shape, 3)
    dma = pltpu.SemaphoreType.DMA
    vmem = pl.BlockSpec(memory_space=pltpu.VMEM)
    out = pl.pallas_call(
        functools.partial(bin_kernel, nz, cuts, groups, tables, shots),
        out_shape=jax.ShapeDtypeStruct((2 * shots, nz * groups * stencil), F32),
        in_specs=[vmem, vmem],
        out_specs=vmem,
        scratch_shapes=[
            pltpu.VMEM((nz,) + value.shape, F32),
            pltpu.VMEM((stencil * 4 * shots, width), BF16),
            pltpu.VMEM((stencil, 2 * shots, nz * groups), F32),
            pltpu.VMEM((nz * groups, stencil, 2 * shots), F32),
            dma((2, nz, len(cuts))),
            dma((2, nz, len(cuts))),
        ],
        name="bin_all",
        compiler_params=pltpu.CompilerParams(
            collective_id=cid, has_side_effects=True, vmem_limit_bytes=56 << 20
        ),
    )(value, weights)
    return out.reshape(2, shots, nz * groups * stencil)


def spread_kernel(ns, in_ref, out_ref, ss, rs, ls):
    c = lax.axis_index("src")
    rows = in_ref.shape[1]
    width = out_ref.shape[2]
    barrier = pltpu.get_barrier_semaphore()
    for off in range(1, ns):
        pl.semaphore_signal(
            barrier, inc=1, device_id={"src": lax.rem(c + off, ns)}, device_id_type=MESH
        )
    pl.semaphore_wait(barrier, ns - 1)

    def part(who, p):
        return in_ref.at[p, :, pl.ds(pl.multiple_of(who * width, 128), width)]

    def place(who, p):
        return out_ref.at[p, pl.ds(pl.multiple_of(who * rows, 8), rows), :]

    sends = []
    for off in range(1, ns):
        for p in (0, 1):
            who = lax.rem(c + off, ns)
            copy = remote(
                part(who, p), place(c, p), ss.at[off - 1, p], rs.at[off - 1, p], {"src": who}
            )
            copy.start()
            sends.append(copy)
    own = [pltpu.make_async_copy(part(c, p), place(c, p), ls.at[p]) for p in (0, 1)]
    for copy in own:
        copy.start()
    for copy in own:
        copy.wait()
    for off in range(1, ns):
        for p in (0, 1):
            who = lax.rem(c + ns - off, ns)
            remote(
                place(who, p), place(who, p), ss.at[off - 1, p], rs.at[off - 1, p], {"src": who}
            ).wait_recv()
    for copy in sends:
        copy.wait_send()


def spread(value, ns, cid):
    _, rows, width = value.shape
    dma = pltpu.SemaphoreType.DMA
    vmem = pl.BlockSpec(memory_space=pltpu.VMEM)
    return pl.pallas_call(
        functools.partial(spread_kernel, ns),
        out_shape=jax.ShapeDtypeStruct((2, ns * rows, width // ns), F32),
        in_specs=[vmem],
        out_specs=vmem,
        scratch_shapes=[dma((ns - 1, 2)), dma((ns - 1, 2)), dma((2,))],
        name="spread",
        compiler_params=pltpu.CompilerParams(collective_id=cid, has_side_effects=True),
    )(value)


def multiply_kernel(
    ns, shots, steps, p_ref, a_ref, out_ref, high, low, mine, give, take, pass_on, got, s1, r1, s2, r2
):
    step = pl.program_id(0)
    c = lax.axis_index("src")
    core = lax.rem(c, 2)
    chip = c // 2
    chips = ns // 2
    half = ns * shots
    tile = a_ref.shape[1]

    @pl.when(step == 0)
    def _():
        barrier = pltpu.get_barrier_semaphore()
        pl.semaphore_signal(barrier, inc=1, device_id={"src": c + 1 - 2 * core}, device_id_type=MESH)
        for off in range(1, chips):
            who = 2 * lax.rem(chip + off, chips) + core
            pl.semaphore_signal(barrier, inc=1, device_id={"src": who}, device_id_type=MESH)
        for part in (0, 1):
            top, rest = split(p_ref[part])
            high[part * half : (part + 1) * half, :] = top
            low[part * half : (part + 1) * half, :] = rest
        pl.semaphore_wait(barrier, chips)

    def to_partner(at):
        return remote(give.at[at], take.at[at], s1.at[at], r1.at[at], {"src": c + 1 - 2 * core})

    def to_chip(at, off):
        who = 2 * lax.rem(chip + off, chips) + core
        return remote(
            pass_on.at[at, off - 1],
            got.at[at, off - 1],
            s2.at[at, off - 1],
            r2.at[at, off - 1],
            {"src": who},
        )

    def reduce_pair(at):
        to_partner(at).wait_recv()
        for off in range(1, chips):
            there = lax.rem(chip + off, chips)
            pass_on[at, off - 1] = mine[at, there] + take[at, there]
            to_chip(at, off).start()
        mine[at, chip] += take[at, chip]

    def times(part):
        top, rest = split(a_ref[part])
        total = lax.dot_general(high[...], top, NT, preferred_element_type=F32)
        total += lax.dot_general(low[...], top, NT, preferred_element_type=F32)
        total += lax.dot_general(high[...], rest, NT, preferred_element_type=F32)
        return total

    by_real = times(0)
    by_imag = times(1)
    both = (by_real[:half] - by_imag[half:], by_imag[:half] + by_real[half:])
    for part in (0, 1):
        for who in range(ns):
            value = both[part][who * shots : (who + 1) * shots]

            @pl.when(core == who % 2)
            def _():
                mine[step, who // 2, part] = value

            @pl.when(core != who % 2)
            def _():
                give[step, who // 2, part] = value

    to_partner(step).start()

    @pl.when(step > 0)
    def _():
        reduce_pair(step - 1)

    @pl.when(step == steps - 1)
    def _():
        reduce_pair(step)
        for at in range(steps):
            total = mine[at, chip]
            for off in range(1, chips):
                to_chip(at, off).wait_recv()
                total += got[at, off - 1]
            out_ref[:, :, at * tile : (at + 1) * tile] = total
        for at in range(steps):
            to_partner(at).wait_send()
            for off in range(1, chips):
                to_chip(at, off).wait_send()


def multiply(columns, aperture, ns, cid):
    _, half, depth = columns.shape
    outs = aperture.shape[1]
    shots = half // ns
    tile = min(outs, 256)
    steps = outs // tile
    chips = ns // 2
    dma = pltpu.SemaphoreType.DMA
    block = (2, shots, tile)
    return pl.pallas_call(
        functools.partial(multiply_kernel, ns, shots, steps),
        grid=(steps,),
        out_shape=jax.ShapeDtypeStruct((2, shots, outs), F32),
        in_specs=[
            pl.BlockSpec(memory_space=pltpu.VMEM),
            pl.BlockSpec((2, tile, depth), lambda i: (0, i, 0)),
        ],
        out_specs=pl.BlockSpec(memory_space=pltpu.VMEM),
        scratch_shapes=[
            pltpu.VMEM((2 * half, depth), BF16),
            pltpu.VMEM((2 * half, depth), BF16),
            pltpu.VMEM((steps, chips) + block, F32),
            pltpu.VMEM((steps, chips) + block, F32),
            pltpu.VMEM((steps, chips) + block, F32),
            pltpu.VMEM((steps, chips - 1) + block, F32),
            pltpu.VMEM((steps, chips - 1) + block, F32),
            dma((steps,)),
            dma((steps,)),
            dma((steps, chips - 1)),
            dma((steps, chips - 1)),
        ],
        name="multiply",
        compiler_params=pltpu.CompilerParams(
            collective_id=cid,
            has_side_effects=True,
            dimension_semantics=("arbitrary",),
            vmem_limit_bytes=56 << 20,
        ),
    )(columns, aperture)


def per_device(nz, ns, traces, moveout, owner, group, table, aperture, shaping):
    groups = aperture.shape[1] // moveout.shape[2]
    shots = traces.shape[0]
    width = traces.shape[2]
    codes = jnp.stack([owner, group, table]).astype(F32)
    codes = jnp.concatenate([codes, jnp.zeros((5, width), F32)])
    flat = jnp.transpose(traces, (1, 0, 2)).reshape(2 * shots, width)
    everyone = bin_all(jnp.concatenate([flat, codes])[None], moveout, nz, groups, shots, 0)
    bins = aperture.shape[1]
    binned = lax.dynamic_slice_in_dim(everyone, lax.axis_index("rcv") * bins, bins, 2)
    form = jnp.transpose(shaping, (1, 0, 2))
    panel = binned
    for sweep in range(ITERS):
        if sweep == 0:
            columns = spread(everyone, ns, 3)
        else:
            columns = gather(panel, nz, ns, True, 8, 1, "gather_panel")
        found = multiply(columns, aperture, ns, 2)
        panel = jnp.stack(
            [
                binned[0] - (form[0] * found[0] - form[1] * found[1]),
                binned[1] - (form[0] * found[1] + form[1] * found[0]),
            ]
        )
    return jnp.transpose(panel, (1, 0, 2))


def solution(mesh):
    nz, ns = mesh.shape["rcv"], mesh.shape["src"]
    in_specs = (
        P(("freq", "src"), None, "rcv"),
        P(None, "freq", None),
        P(("freq", "rcv")),
        P(("freq", "rcv")),
        P(("freq", "rcv")),
        P(None, ("freq", "rcv"), "src"),
        P(("freq", "src"), None, "rcv"),
    )
    out_specs = P(("freq", "src"), None, "rcv")
    return jax.shard_map(
        functools.partial(per_device, nz, ns),
        mesh=mesh,
        in_specs=in_specs,
        out_specs=out_specs,
        check_vma=False,
    )
```

profile of v0, /device:TPU:0, one launch (start us, length us, event | category | flops | bytes accessed | tf_op | source)
XLA Modules:
  0.0 164.8 jit_solution(3329640570147301910)
XLA Ops:
  0.0 0.1 pad.6.clone
  0.1 0.7 add_convert_fusion
  0.8 1.0 copy.8
  1.9 0.8 maximum_bitcast_fusion.1.in_ref
  2.7 1.3 copy.12
  4.0 33.1 %bin_all.1 = f32[64,8192]{1,0:T(8,128)} custom-call(f32[1,72,1024]{2,1,0:T(8,128)} %maximum_bitcast_fusion.1.in_ref, f32[32,32]{1,0:T(8,128)} %bitcast.23), custom_call_target="tpu_custom_call" | custom-call | tf_op jit(solution)/shard_map/bin_all/pallas_call | solution.py:335
  37.1 27.5 %spread.1.p_ref = f32[2,128,2048]{2,1,0:T(8,128)} custom-call(f32[2,32,8192]{2,1,0:T(8,128)} %bitcast.16), custom_call_target="tpu_custom_call" | custom-call | tf_op jit(solution)/shard_map/spread/pallas_call | solution.py:401
  64.6 0.0 copy-start
  64.6 26.8 %multiply.2 = f32[2,32,2048]{2,1,0:T(8,128)} custom-call(f32[2,128,2048]{2,1,0:T(8,128)} %spread.1.p_ref, f32[2,2048,2048]{2,1,0:T(8,128)} %a_ref.3), custom_call_target="tpu_custom_call" | custom-call | tf_op jit(solution)/shard_map/multiply/pallas_call | solution.py:509
  91.4 0.0 copy-done
  91.4 1.1 subtract_subtract_fusion.1
  92.5 0.8 pad_maximum_fusion.in_ref
  93.4 42.4 %gather_panel.1.p_ref = f32[2,128,2048]{2,1,0:T(8,128)} custom-call(f32[2,32,2048]{2,1,0:T(8,128)} %pad_maximum_fusion.in_ref), custom_call_target="tpu_custom_call" | custom-call | tf_op jit(solution)/shard_map/gather_panel/pallas_call | solution.py:201
  135.8 26.6 %multiply.3 = f32[2,32,2048]{2,1,0:T(8,128)} custom-call(f32[2,128,2048]{2,1,0:T(8,128)} %gather_panel.1.p_ref, f32[2,2048,2048]{2,1,0:T(8,128)} %a_ref.3), custom_call_target="tpu_custom_call" | custom-call | tf_op jit(solution)/shard_map/multiply/pallas_call | solution.py:509
  162.4 1.1 subtract_subtract_fusion
  163.6 1.2 copy.10
  (2 shorter events, 0.0 us)
Async XLA Ops:
  64.6 26.8 %copy-start = (f32[64,8192]{1,0:T(8,128)S(1)}, f32[64,8192]{1,0:T(8,128)}, u32[]{:S(2)}) copy-start(f32[64,8192]{1,0:T(8,128)} %bin_all.1) | copy-start | bytes 6291460
where the time goes:
time: 165 us
  Pallas kernels  156 us (95%)
  other arithmetic  4.64 us (3%)
  local copies, waits for them, and re-layouts  3.67 us (2%)
    pallas_call x2, Pallas kernels, multiply(): pl.pallas_call(functools.partial(multiply_kernel, ns, shots, steps), grid...  53.4 us
    pallas_call x1, Pallas kernels, gather(): pl.pallas_call(functools.partial(gather_kernel, nz, ns, fold, plane, cuts...  42.4 us
    pallas_call x1, Pallas kernels, bin_all(): pl.pallas_call(functools.partial(bin_kernel, nz, cuts, groups, tables, sh...  33.1 us
    pallas_call x1, Pallas kernels, spread(): pl.pallas_call(functools.partial(spread_kernel, ns), out_shape=jax.ShapeD...  27.5 us

commit v1 on v0

v1 whole, which is shorter than its diff:
```python
import functools

import jax
import jax.numpy as jnp
from jax import lax
from jax.experimental import pallas as pl
from jax.experimental.pallas import tpu as pltpu
from jax.sharding import PartitionSpec as P

ITERS = 2
MESH = pl.DeviceIdType.MESH
F32 = jnp.float32
BF16 = jnp.bfloat16
NT = (((1,), (1,)), ((), ()))


def split(value):
    high = value.astype(BF16)
    return high, (value - high.astype(F32)).astype(BF16)


def remote(src, dst, send_sem, recv_sem, where):
    return pltpu.make_async_remote_copy(
        src_ref=src,
        dst_ref=dst,
        send_sem=send_sem,
        recv_sem=recv_sem,
        device_id=where,
        device_id_type=MESH,
    )


def pieces(refs_shape, count):
    planes, rows = refs_shape[0], refs_shape[1]
    per = max(1, count // planes)
    step = rows // per
    return [(p, pl.ds(h * step, step)) for p in range(planes) for h in range(per)]


def bin_kernel(
    nz, cuts, groups, tables, shots, in_ref, wt_ref, out_ref, held, terms, total, order, zs, zr
):
    z = lax.axis_index("rcv")
    stencil = wt_ref.shape[0] // 2
    rows = 2 * shots
    width = in_ref.shape[-1]
    cells = nz * groups

    def has(lane):
        near = z + 1 - 2 * lane
        return (near >= 0) & (near < nz)

    barrier = pltpu.get_barrier_semaphore()
    for lane in (0, 1):

        @pl.when(has(lane))
        def _():
            pl.semaphore_signal(
                barrier, inc=1, device_id={"rcv": z + 1 - 2 * lane}, device_id_type=MESH
            )

    pl.semaphore_wait(barrier, jnp.where(z > 0, 1, 0) + jnp.where(z < nz - 1, 1, 0))

    def along(own, block, lane, dist, q):
        cut = cuts[q]
        return remote(
            in_ref.at[cut] if own else held.at[(block,) + cut],
            held.at[(block,) + cut],
            zs.at[lane, dist, q],
            zr.at[lane, dist, q],
            {"rcv": z + 1 - 2 * lane},
        )

    for q in range(len(cuts)):
        for lane in (0, 1):

            @pl.when(has(lane))
            def _():
                along(True, z, lane, 0, q).start()

    w = wt_ref[...]
    w0 = w.astype(BF16)
    rest = w - w0.astype(F32)
    w1 = rest.astype(BF16)
    w2 = (rest - w1.astype(F32)).astype(BF16)
    table_ids = lax.broadcasted_iota(jnp.int32, (tables, width), 0).astype(F32)
    cell_ids = lax.broadcasted_iota(jnp.int32, (cells, width), 0).astype(F32)

    def sums(view):
        cell = view[0, rows : rows + 1, :] * float(groups) + view[0, rows + 1 : rows + 2, :]
        table_hot = (table_ids == view[0, rows + 2 : rows + 3, :]).astype(BF16)
        picked = sum(
            jnp.dot(part, table_hot, preferred_element_type=F32) for part in (w0, w1, w2)
        )
        hot = (cell_ids == cell).astype(BF16)
        real = view[0, 0:shots, :]
        imag = view[0, shots:rows, :]
        for j in range(stencil):
            wr = picked[j : j + 1, :]
            wi = picked[stencil + j : stencil + j + 1, :]
            base = j * 2 * rows
            for part, both in enumerate((real * wr - imag * wi, real * wi + imag * wr)):
                high, low = split(both)
                at = base + part * shots
                terms[at : at + shots, :] = high
                terms[at + rows : at + rows + shots, :] = low
        found = lax.dot_general(terms[...], hot, NT, preferred_element_type=F32)
        found = found.reshape(stencil, 2, rows, cells)
        return found[:, 0] + found[:, 1]

    total[...] = sums(in_ref)

    def hop(dist, carry):
        for q in range(len(cuts)):
            for lane in (0, 1):
                block = z - dist * (1 - 2 * lane)

                @pl.when((block >= 0) & (block < nz))
                def _():
                    along(False, block, lane, dist - 1, q).wait_recv()

                    @pl.when(has(lane))
                    def _():
                        along(False, block, lane, dist, q).start()

        def add(lane, inner):
            block = z - dist * (1 - 2 * lane)

            @pl.when((block >= 0) & (block < nz))
            def _():
                total[...] += sums(held.at[block])

            return inner

        return lax.fori_loop(0, 2, add, carry)

    lax.fori_loop(1, nz, hop, 0)
    for j in range(stencil):
        order[:, j, :] = total[j].T
    out_ref[...] = order[...].reshape(cells * stencil, rows).T

    def drain(dist, carry):
        for q in range(len(cuts)):
            for lane in (0, 1):
                block = z - dist * (1 - 2 * lane)

                @pl.when((block >= 0) & (block < nz) & has(lane))
                def _():
                    along(False, block, lane, dist, q).wait_send()

        return carry

    lax.fori_loop(0, nz, drain, 0)


def bin_all(value, moveout, nz, groups, shots, cid):
    tables, stencil = moveout.shape[1:]
    width = value.shape[-1]
    weights = jnp.transpose(moveout, (0, 2, 1)).reshape(2 * stencil, tables)
    cuts = pieces(value.shape, 3)
    dma = pltpu.SemaphoreType.DMA
    vmem = pl.BlockSpec(memory_space=pltpu.VMEM)
    out = pl.pallas_call(
        functools.partial(bin_kernel, nz, cuts, groups, tables, shots),
        out_shape=jax.ShapeDtypeStruct((2 * shots, nz * groups * stencil), F32),
        in_specs=[vmem, vmem],
        out_specs=vmem,
        scratch_shapes=[
            pltpu.VMEM((nz,) + value.shape, F32),
            pltpu.VMEM((stencil * 4 * shots, width), BF16),
            pltpu.VMEM((stencil, 2 * shots, nz * groups), F32),
            pltpu.VMEM((nz * groups, stencil, 2 * shots), F32),
            dma((2, nz, len(cuts))),
            dma((2, nz, len(cuts))),
        ],
        name="bin_all",
        compiler_params=pltpu.CompilerParams(
            collective_id=cid, has_side_effects=True, vmem_limit_bytes=56 << 20
        ),
    )(value, weights)
    return out.reshape(2, shots, nz * groups * stencil)


def spread_kernel(ns, in_ref, out_ref, ss, rs, ls):
    c = lax.axis_index("src")
    rows = in_ref.shape[1]
    width = out_ref.shape[2]
    barrier = pltpu.get_barrier_semaphore()
    for off in range(1, ns):
        pl.semaphore_signal(
            barrier, inc=1, device_id={"src": lax.rem(c + off, ns)}, device_id_type=MESH
        )
    pl.semaphore_wait(barrier, ns - 1)

    def part(who, p):
        return in_ref.at[p, :, pl.ds(pl.multiple_of(who * width, 128), width)]

    def place(who, p):
        return out_ref.at[p, pl.ds(pl.multiple_of(who * rows, 8), rows), :]

    sends = []
    for off in range(1, ns):
        for p in (0, 1):
            who = lax.rem(c + off, ns)
            copy = remote(
                part(who, p), place(c, p), ss.at[off - 1, p], rs.at[off - 1, p], {"src": who}
            )
            copy.start()
            sends.append(copy)
    own = [pltpu.make_async_copy(part(c, p), place(c, p), ls.at[p]) for p in (0, 1)]
    for copy in own:
        copy.start()
    for copy in own:
        copy.wait()
    for off in range(1, ns):
        for p in (0, 1):
            who = lax.rem(c + ns - off, ns)
            remote(
                place(who, p), place(who, p), ss.at[off - 1, p], rs.at[off - 1, p], {"src": who}
            ).wait_recv()
    for copy in sends:
        copy.wait_send()


def spread(value, ns, cid):
    _, rows, width = value.shape
    dma = pltpu.SemaphoreType.DMA
    vmem = pl.BlockSpec(memory_space=pltpu.VMEM)
    return pl.pallas_call(
        functools.partial(spread_kernel, ns),
        out_shape=jax.ShapeDtypeStruct((2, ns * rows, width // ns), F32),
        in_specs=[vmem],
        out_specs=vmem,
        scratch_shapes=[dma((ns - 1, 2)), dma((ns - 1, 2)), dma((2,))],
        name="spread",
        compiler_params=pltpu.CompilerParams(collective_id=cid, has_side_effects=True),
    )(value)


def sweeps_kernel(
    nz, ns, shots, tile, steps, fold,
    p_ref, b_ref, f_ref, a_ref, out_ref,
    a_all, high, low, mine, give, take, pass_on, got, own, held, cols, acc,
    a_sem, s1, r1, s2, r2, zs, zr, ps, pr, ls,
):
    z = lax.axis_index("rcv")
    c = lax.axis_index("src")
    core = lax.rem(c, 2)
    chip = c // 2
    chips = ns // 2
    half = ns * shots
    outs = steps * tile
    early = steps // 2
    last = steps + 1

    def a_copy(t):
        rows = pl.ds(pl.multiple_of(t * tile, tile), tile)
        return pltpu.make_async_copy(a_ref.at[:, rows, :], a_all.at[:, rows, :], a_sem.at[t])

    for t in range(min(2, steps)):
        a_copy(t).start()

    def has(lane):
        near = z + 1 - 2 * lane
        return (near >= 0) & (near < nz)

    barrier = pltpu.get_barrier_semaphore()
    for lane in (0, 1):

        @pl.when(has(lane))
        def _():
            pl.semaphore_signal(
                barrier, inc=1, device_id={"rcv": z + 1 - 2 * lane}, device_id_type=MESH
            )

    for off in range(1, ns):
        pl.semaphore_signal(
            barrier, inc=1, device_id={"src": lax.rem(c + off, ns)}, device_id_type=MESH
        )
    for part in (0, 1):
        top, rest = split(p_ref[part])
        high[part * half : (part + 1) * half, :] = top
        low[part * half : (part + 1) * half, :] = rest
    peers = jnp.where(z > 0, 1, 0) + jnp.where(z < nz - 1, 1, 0)
    pl.semaphore_wait(barrier, peers + ns - 1)

    def to_partner(sweep, t):
        return remote(
            give.at[sweep, t],
            take.at[sweep, t],
            s1.at[sweep, t],
            r1.at[sweep, t],
            {"src": c + 1 - 2 * core},
        )

    def to_chip(sweep, t, off):
        who = 2 * lax.rem(chip + off, chips) + core
        return remote(
            pass_on.at[sweep, t, off - 1],
            got.at[sweep, t, off - 1],
            s2.at[sweep, t, off - 1],
            r2.at[sweep, t, off - 1],
            {"src": who},
        )

    def times(t, ranges):
        rows = pl.ds(pl.multiple_of(t * tile, tile), tile)
        sums = []
        for part in (0, 1):
            total = None
            for cut in ranges:
                top, rest = split(a_all[part, rows, cut])
                now = lax.dot_general(high[:, cut], top, NT, preferred_element_type=F32)
                now += lax.dot_general(low[:, cut], top, NT, preferred_element_type=F32)
                now += lax.dot_general(high[:, cut], rest, NT, preferred_element_type=F32)
                total = now if total is None else total + now
            sums.append(total)
        return sums[0][:half] - sums[1][half:], sums[1][:half] + sums[0][half:]

    def hand_out(sweep, t, both):
        for part in (0, 1):
            for who in range(ns):
                value = both[part][who * shots : (who + 1) * shots]

                @pl.when(core == who % 2)
                def _():
                    mine[sweep, t, who // 2, part] = value

                @pl.when(core != who % 2)
                def _():
                    give[sweep, t, who // 2, part] = value

        to_partner(sweep, t).start()

    def reduce_pair(sweep, t):
        to_partner(sweep, t).wait_recv()
        for off in range(1, chips):
            there = lax.rem(chip + off, chips)
            pass_on[sweep, t, off - 1] = mine[sweep, t, there] + take[sweep, t, there]
            to_chip(sweep, t, off).start()
        mine[sweep, t, chip] += take[sweep, t, chip]

    def finish(sweep, t):
        found = mine[sweep, t, chip]
        for off in range(1, chips):
            to_chip(sweep, t, off).wait_recv()
            found += got[sweep, t, off - 1]
        at = pl.ds(pl.multiple_of(t * tile, tile), tile)
        fr, fi = f_ref[0, :, at], f_ref[1, :, at]
        return (
            b_ref[0, :, at] - (fr * found[0] - fi * found[1]),
            b_ref[1, :, at] - (fr * found[1] + fi * found[0]),
        )

    def along(src, block, lane, dist, t):
        return remote(
            src,
            held.at[block, t],
            zs.at[lane, dist, t],
            zr.at[lane, dist, t],
            {"rcv": z + 1 - 2 * lane},
        )

    def across(src, block, t):
        f = block - (block // fold) * fold
        return remote(
            src, cols.at[f, t, c], ps.at[block, t], pr.at[c, f, t], {"src": block // fold}
        )

    def local(src, block, t):
        f = block - (block // fold) * fold
        return pltpu.make_async_copy(src, cols.at[f, t, c], ls.at[f, t])

    def hand_on(src, block, t):
        @pl.when(block // fold != c)
        def _():
            across(src, block, t).start()

        @pl.when(block // fold == c)
        def _():
            local(src, block, t).start()

    def relay(t, dist):
        for lane in (0, 1):
            block = z - dist * (1 - 2 * lane)

            @pl.when((block >= 0) & (block < nz))
            def _():
                along(held.at[block, t], block, lane, dist - 1, t).wait_recv()

                @pl.when(has(lane))
                def _():
                    along(held.at[block, t], block, lane, dist, t).start()

                hand_on(held.at[block, t], block, t)

    def first(step, carry):
        @pl.when(step < steps)
        def _():
            a_copy(step).wait()

            @pl.when(step + 2 < steps)
            def _():
                a_copy(step + 2).start()

            hand_out(0, step, times(step, [pl.ds(0, fold * outs)]))

        @pl.when((step >= 1) & (step <= steps))
        def _():
            reduce_pair(0, step - 1)

        @pl.when(step >= 2)
        def _():
            t = step - 2
            real, imag = finish(0, t)
            own[t, 0] = real
            own[t, 1] = imag
            for lane in (0, 1):

                @pl.when(has(lane))
                def _():
                    along(own.at[t], z, lane, 0, t).start()

            hand_on(own.at[t], z, t)

        def earlier(dist, inner):
            t = step - 2 - 2 * dist

            @pl.when(t >= 0)
            def _():
                relay(t, dist)

            return inner

        return lax.fori_loop(1, nz, earlier, carry)

    lax.fori_loop(0, last + 1, first, 0)

    def rest_of(t):
        def each(dist, carry):
            @pl.when(t + 2 + 2 * dist > last)
            def _():
                relay(t, dist)

            return carry

        lax.fori_loop(1, nz, each, 0)

    def take_in(t, carry):
        for f in range(fold):
            local(own.at[t], c * fold + f, t).wait()
            for off in range(1, ns):
                who = lax.rem(c + off, ns)
                remote(
                    cols.at[f, t, who],
                    cols.at[f, t, who],
                    ps.at[0, t],
                    pr.at[who, f, t],
                    {"src": who},
                ).wait_recv()
            at = pl.ds(pl.multiple_of(f * outs + t * tile, tile), tile)
            for part in (0, 1):
                top, rest = split(cols[f, t, :, part].reshape(half, tile))
                high[part * half : (part + 1) * half, at] = top
                low[part * half : (part + 1) * half, at] = rest
        return carry

    def range_of(start, size):
        return [pl.ds(f * outs + start * tile, size * tile) for f in range(fold)]

    for t in range(early):
        rest_of(t)
    lax.fori_loop(0, early, take_in, 0)
    share = -(-steps // (steps - early))

    def between(t, carry):
        rest_of(t)

        def some(i, inner):
            r = (t - early) * share + i

            @pl.when(r < steps)
            def _():
                real, imag = times(r, range_of(0, early))
                acc[r, 0] = real
                acc[r, 1] = imag

            return inner

        return lax.fori_loop(0, share, some, carry)

    lax.fori_loop(early, steps, between, 0)
    lax.fori_loop(early, steps, take_in, 0)

    def second(step, carry):
        @pl.when(step < steps)
        def _():
            real, imag = times(step, range_of(early, steps - early))
            hand_out(1, step, (real + acc[step, 0], imag + acc[step, 1]))

        @pl.when((step >= 1) & (step <= steps))
        def _():
            reduce_pair(1, step - 1)

        @pl.when(step >= 2)
        def _():
            t = step - 2
            real, imag = finish(1, t)
            at = pl.ds(pl.multiple_of(t * tile, tile), tile)
            out_ref[0, :, at] = real
            out_ref[1, :, at] = imag

        return carry

    lax.fori_loop(0, last + 1, second, 0)

    def drain(t, carry):
        for sweep in (0, 1):
            to_partner(sweep, t).wait_send()
            for off in range(1, chips):
                to_chip(sweep, t, off).wait_send()

        def each(dist, inner):
            for lane in (0, 1):
                block = z - dist * (1 - 2 * lane)

                @pl.when((block >= 0) & (block < nz) & has(lane))
                def _():
                    along(held.at[block, t], block, lane, dist, t).wait_send()

            @pl.when(dist // fold != c)
            def _():
                across(held.at[dist, t], dist, t).wait_send()

            return inner

        return lax.fori_loop(0, nz, each, carry)

    lax.fori_loop(0, steps, drain, 0)


def two_sweeps(columns, binned, form, aperture, nz, ns, cid):
    _, half, depth = columns.shape
    outs = aperture.shape[1]
    shots = half // ns
    tile = min(outs, 256)
    steps = outs // tile
    chips = ns // 2
    fold = depth // outs
    dma = pltpu.SemaphoreType.DMA
    vmem = pl.BlockSpec(memory_space=pltpu.VMEM)
    block = (2, shots, tile)
    return pl.pallas_call(
        functools.partial(sweeps_kernel, nz, ns, shots, tile, steps, fold),
        out_shape=jax.ShapeDtypeStruct((2, shots, outs), F32),
        in_specs=[vmem, vmem, vmem, pl.BlockSpec(memory_space=pl.ANY)],
        out_specs=vmem,
        scratch_shapes=[
            pltpu.VMEM((2, outs, depth), F32),
            pltpu.VMEM((2 * half, depth), BF16),
            pltpu.VMEM((2 * half, depth), BF16),
            pltpu.VMEM((ITERS, steps, chips) + block, F32),
            pltpu.VMEM((ITERS, steps, chips) + block, F32),
            pltpu.VMEM((ITERS, steps, chips) + block, F32),
            pltpu.VMEM((ITERS, steps, chips - 1) + block, F32),
            pltpu.VMEM((ITERS, steps, chips - 1) + block, F32),
            pltpu.VMEM((steps,) + block, F32),
            pltpu.VMEM((nz, steps) + block, F32),
            pltpu.VMEM((fold, steps, ns) + block, F32),
            pltpu.VMEM((steps, 2, half, tile), F32),
            dma((steps,)),
            dma((ITERS, steps)),
            dma((ITERS, steps)),
            dma((ITERS, steps, chips - 1)),
            dma((ITERS, steps, chips - 1)),
            dma((2, nz, steps)),
            dma((2, nz, steps)),
            dma((nz, steps)),
            dma((ns, fold, steps)),
            dma((fold, steps)),
        ],
        name="two_sweeps",
        compiler_params=pltpu.CompilerParams(
            collective_id=cid, has_side_effects=True, vmem_limit_bytes=62 << 20
        ),
    )(columns, binned, form, aperture)


def per_device(nz, ns, traces, moveout, owner, group, table, aperture, shaping):
    groups = aperture.shape[1] // moveout.shape[2]
    shots = traces.shape[0]
    width = traces.shape[2]
    codes = jnp.stack([owner, group, table]).astype(F32)
    codes = jnp.concatenate([codes, jnp.zeros((5, width), F32)])
    flat = jnp.transpose(traces, (1, 0, 2)).reshape(2 * shots, width)
    everyone = bin_all(jnp.concatenate([flat, codes])[None], moveout, nz, groups, shots, 0)
    bins = aperture.shape[1]
    binned = lax.dynamic_slice_in_dim(everyone, lax.axis_index("rcv") * bins, bins, 2)
    form = jnp.transpose(shaping, (1, 0, 2))
    columns = spread(everyone, ns, 3)
    panel = two_sweeps(columns, binned, form, aperture, nz, ns, 2)
    return jnp.transpose(panel, (1, 0, 2))


def solution(mesh):
    nz, ns = mesh.shape["rcv"], mesh.shape["src"]
    in_specs = (
        P(("freq", "src"), None, "rcv"),
        P(None, "freq", None),
        P(("freq", "rcv")),
        P(("freq", "rcv")),
        P(("freq", "rcv")),
        P(None, ("freq", "rcv"), "src"),
        P(("freq", "src"), None, "rcv"),
    )
    out_specs = P(("freq", "src"), None, "rcv")
    return jax.shard_map(
        functools.partial(per_device, nz, ns),
        mesh=mesh,
        in_specs=in_specs,
        out_specs=out_specs,
        check_vma=False,
    )
```

time: 165 us -> 151 us (0.915)
  Pallas kernels: 156 us -> 143 us
  other arithmetic: 4.64 us -> 1.54 us
  local copies, waits for them, and re-layouts: 3.67 us -> 6.34 us
    pallas_call x3 -> x1, Pallas kernels: 95.8 us -> 82 us  [two_sweeps(): pl.pallas_call(functools.partial(sweeps_kernel, nz, ns, shots, tile, step...]
    sub x2 -> x0, other arithmetic: 2.24 us -> none  [per_device(): binned[0] - (form[0] * found[0] - form[1] * found[1])]
    dynamic_slice x0 -> x1, local copies, waits for them, and re-layouts: none -> 1.88 us  [per_device(): lax.dynamic_slice_in_dim(everyone, lax.axis_index('rcv') * bins, bins, 2)]
where the time goes in v1:
time: 151 us
  Pallas kernels  143 us (95%)
  local copies, waits for them, and re-layouts  6.34 us (4%)
  other arithmetic  1.54 us (1%)
    pallas_call x1, Pallas kernels, two_sweeps(): pl.pallas_call(functools.partial(sweeps_kernel, nz, ns, shots, tile, step...  82 us
    pallas_call x1, Pallas kernels, bin_all(): pl.pallas_call(functools.partial(bin_kernel, nz, cuts, groups, tables, sh...  33 us
    pallas_call x1, Pallas kernels, spread(): pl.pallas_call(functools.partial(spread_kernel, ns), out_shape=jax.ShapeD...  27.6 us

profile of v1, /device:TPU:0, one launch (start us, length us, event | category | flops | bytes accessed | tf_op | source)
XLA Modules:
  0.0 150.6 jit_solution(10133609290013783360)
XLA Ops:
  0.0 1.0 copy.8
  1.0 0.7 add_convert_fusion
  1.8 0.1 pad.2.clone
  1.9 0.8 maximum_bitcast_fusion.in_ref
  2.7 33.0 %bin_all.1 = f32[64,8192]{1,0:T(8,128)} custom-call(f32[1,72,1024]{2,1,0:T(8,128)} %maximum_bitcast_fusion.in_ref, f32[32,32]{1,0:T(8,128)} %bitcast.21), custom_call_target="tpu_custom_call" | custom-call | tf_op jit(solution)/shard_map/bin_all/pallas_call | solution.py:163
  35.7 1.9 %constant_dynamic-slice_fusion.b_ref = f32[2,32,2048]{2,1,0:T(8,128)} fusion(f32[2,32,8192]{2,1,0:T(8,128)} %bitcast.15, s32[]{:T(128)S(6)} %select_n.3), kind=kLoop, calls=%fused_computation.3 | loop fusion | bytes 1048580 | tf_op jit(solution)/shard_map/dynamic_slice | solution.py:598
  37.6 0.0 copy-start
  37.6 27.6 %spread.1.p_ref = f32[2,128,2048]{2,1,0:T(8,128)} custom-call(f32[2,32,8192]{2,1,0:T(8,128)} %bitcast.16), custom_call_target="tpu_custom_call" | custom-call | tf_op jit(solution)/shard_map/spread/pallas_call | solution.py:229
  65.2 0.0 copy-done
  65.2 1.1 copy.12
  66.3 82.0 %two_sweeps.1 = f32[2,32,2048]{2,1,0:T(8,128)} custom-call(f32[2,128,2048]{2,1,0:T(8,128)} %spread.1.p_ref, f32[2,32,2048]{2,1,0:T(8,128)} %constant_dynamic-slice_fusion.b_ref, f32[2,32,2048]{2,1,0:T(8,128)} %bitcast.18, f32[2,2048,2048]{2,1,0:T(8,128)} %a_ref.1), custom_call_target="tpu_custom_call" | custom-call | tf_op jit(solution)/shard_map/two_sweeps/pallas_call | solution.py:553
  148.3 2.2 %copy.10 = f32[32,2,2048]{2,1,0:T(2,128)} copy(f32[32,2,2048]{2,0,1:T(8,128)} %bitcast.17) | data formatting | bytes 1048576 | tf_op jit(solution)/shard_map/transpose | solution.py:602
  (1 shorter events, 0.0 us)
Async XLA Ops:
  37.6 27.6 %copy-start = (f32[32,2,2048]{2,1,0:T(2,128)S(1)}, f32[32,2,2048]{2,1,0:T(2,128)}, u32[]{:S(2)}) copy-start(f32[32,2,2048]{2,1,0:T(2,128)} %param.13) | copy-start | bytes 1572868

commit v2 on v1

--- a/solution.py
+++ b/solution.py
@@ -8,6 +8,12 @@
 from jax.sharding import PartitionSpec as P
 
 ITERS = 2
+SUB = 8
+LANES = 128
+SOON = 4
+LAG = 3
+HOP = 1
+BEHIND = 4
 MESH = pl.DeviceIdType.MESH
 F32 = jnp.float32
 BF16 = jnp.bfloat16
@@ -30,21 +36,20 @@
     )
 
 
-def pieces(refs_shape, count):
-    planes, rows = refs_shape[0], refs_shape[1]
-    per = max(1, count // planes)
-    step = rows // per
-    return [(p, pl.ds(h * step, step)) for p in range(planes) for h in range(per)]
-
-
 def bin_kernel(
-    nz, cuts, groups, tables, shots, in_ref, wt_ref, out_ref, held, terms, total, order, zs, zr
+    nz, ns, groups, tables, fold,
+    tr_ref, ow_ref, gr_ref, tb_ref, wt_ref, p_ref, b_ref,
+    codes, held, hot, picked, terms, sums, got, order, order_own,
+    cs, cr, zs, zr, ss, rs, ls,
 ):
     z = lax.axis_index("rcv")
+    c = lax.axis_index("src")
+    shots, _, width = tr_ref.shape
     stencil = wt_ref.shape[0] // 2
-    rows = 2 * shots
-    width = in_ref.shape[-1]
+    chunks = shots // SUB
     cells = nz * groups
+    share = cells // ns
+    half = ns * shots
 
     def has(lane):
         near = z + 1 - 2 * lane
@@ -59,88 +64,184 @@
                 barrier, inc=1, device_id={"rcv": z + 1 - 2 * lane}, device_id_type=MESH
             )
 
-    pl.semaphore_wait(barrier, jnp.where(z > 0, 1, 0) + jnp.where(z < nz - 1, 1, 0))
+    for off in range(1, ns):
+        pl.semaphore_signal(
+            barrier, inc=1, device_id={"src": lax.rem(c + off, ns)}, device_id_type=MESH
+        )
+    codes[z, 0:1] = ow_ref[...]
+    codes[z, 1:2] = gr_ref[...]
+    codes[z, 2:3] = tb_ref[...]
+    peers = jnp.where(z > 0, 1, 0) + jnp.where(z < nz - 1, 1, 0)
+    pl.semaphore_wait(barrier, peers + ns - 1)
+
+    def span(q):
+        return pl.ds(pl.multiple_of(q * SUB, SUB), SUB)
 
     def along(own, block, lane, dist, q):
-        cut = cuts[q]
         return remote(
-            in_ref.at[cut] if own else held.at[(block,) + cut],
-            held.at[(block,) + cut],
+            tr_ref.at[span(q)] if own else held.at[block, span(q)],
+            held.at[block, span(q)],
             zs.at[lane, dist, q],
             zr.at[lane, dist, q],
             {"rcv": z + 1 - 2 * lane},
         )
 
-    for q in range(len(cuts)):
-        for lane in (0, 1):
-
-            @pl.when(has(lane))
-            def _():
-                along(True, z, lane, 0, q).start()
+    def code(block, lane, dist):
+        return remote(
+            codes.at[block],
+            codes.at[block],
+            cs.at[lane, dist],
+            cr.at[lane, dist],
+            {"rcv": z + 1 - 2 * lane},
+        )
+
+    def columns(block):
+        return pl.ds(pl.multiple_of(block * width, width), width)
 
     w = wt_ref[...]
     w0 = w.astype(BF16)
     rest = w - w0.astype(F32)
     w1 = rest.astype(BF16)
     w2 = (rest - w1.astype(F32)).astype(BF16)
-    table_ids = lax.broadcasted_iota(jnp.int32, (tables, width), 0).astype(F32)
-    cell_ids = lax.broadcasted_iota(jnp.int32, (cells, width), 0).astype(F32)
-
-    def sums(view):
-        cell = view[0, rows : rows + 1, :] * float(groups) + view[0, rows + 1 : rows + 2, :]
-        table_hot = (table_ids == view[0, rows + 2 : rows + 3, :]).astype(BF16)
-        picked = sum(
+    table_ids = lax.broadcasted_iota(jnp.int32, (tables, width), 0)
+    cell_ids = lax.broadcasted_iota(jnp.int32, (cells, width), 0)
+
+    def prepare(block):
+        at = columns(block)
+        cell = codes[block, 0:1] * groups + codes[block, 1:2]
+        hot[:, at] = jnp.where(cell_ids == cell, 1.0, 0.0).astype(BF16)
+        table_hot = jnp.where(table_ids == codes[block, 2:3], 1.0, 0.0).astype(BF16)
+        picked[:, at] = sum(
             jnp.dot(part, table_hot, preferred_element_type=F32) for part in (w0, w1, w2)
         )
-        hot = (cell_ids == cell).astype(BF16)
-        real = view[0, 0:shots, :]
-        imag = view[0, shots:rows, :]
+
+    def spread_terms(real, imag, block):
+        at = columns(block)
         for j in range(stencil):
-            wr = picked[j : j + 1, :]
-            wi = picked[stencil + j : stencil + j + 1, :]
-            base = j * 2 * rows
-            for part, both in enumerate((real * wr - imag * wi, real * wi + imag * wr)):
-                high, low = split(both)
-                at = base + part * shots
-                terms[at : at + shots, :] = high
-                terms[at + rows : at + rows + shots, :] = low
-        found = lax.dot_general(terms[...], hot, NT, preferred_element_type=F32)
-        found = found.reshape(stencil, 2, rows, cells)
-        return found[:, 0] + found[:, 1]
-
-    total[...] = sums(in_ref)
-
-    def hop(dist, carry):
-        for q in range(len(cuts)):
+            wr = picked[j : j + 1, at]
+            wi = picked[stencil + j : stencil + j + 1, at]
+            both = jnp.concatenate([real * wr - imag * wi, real * wi + imag * wr])
+            high, low = split(both)
+            base = j * 4 * SUB
+            terms[base : base + 2 * SUB, at] = high
+            terms[base + 2 * SUB : base + 4 * SUB, at] = low
+
+    def across(q, who):
+        return remote(sums.at[q, who], got.at[q, c], ss.at[q, who], rs.at[q, c], {"src": who})
+
+    def keep(q):
+        return pltpu.make_async_copy(sums.at[q, c], got.at[q, c], ls.at[q])
+
+    def chunk(q, carry):
+        @pl.when(q == 0)
+        def _():
+            for lane in (0, 1):
+
+                @pl.when(has(lane))
+                def _():
+                    code(z, lane, 0).start()
+                    along(True, z, lane, 0, 0).start()
+
+        @pl.when(q + 1 < chunks)
+        def _():
+            for lane in (0, 1):
+
+                @pl.when(has(lane))
+                def _():
+                    along(True, z, lane, 0, q + 1).start()
+
+        @pl.when(q == 0)
+        def _():
+            prepare(z)
+
+        spread_terms(tr_ref[span(q), 0, :], tr_ref[span(q), 1, :], z)
+
+        def hop(dist, inner):
             for lane in (0, 1):
                 block = z - dist * (1 - 2 * lane)
 
                 @pl.when((block >= 0) & (block < nz))
                 def _():
+                    @pl.when(q == 0)
+                    def _():
+                        code(block, lane, dist - 1).wait_recv()
+
+                        @pl.when(has(lane))
+                        def _():
+                            code(block, lane, dist).start()
+
                     along(False, block, lane, dist - 1, q).wait_recv()
 
                     @pl.when(has(lane))
                     def _():
                         along(False, block, lane, dist, q).start()
 
-        def add(lane, inner):
-            block = z - dist * (1 - 2 * lane)
-
-            @pl.when((block >= 0) & (block < nz))
-            def _():
-                total[...] += sums(held.at[block])
-
-            return inner
-
-        return lax.fori_loop(0, 2, add, carry)
-
-    lax.fori_loop(1, nz, hop, 0)
+            def add(lane, deeper):
+                block = z - dist * (1 - 2 * lane)
+
+                @pl.when((block >= 0) & (block < nz))
+                def _():
+                    @pl.when(q == 0)
+                    def _():
+                        prepare(block)
+
+                    spread_terms(held[block, span(q), 0, :], held[block, span(q), 1, :], block)
+
+                return deeper
+
+            return lax.fori_loop(0, 2, add, inner)
+
+        lax.fori_loop(1, nz, hop, 0)
+        found = lax.dot_general(terms[...], hot[...], NT, preferred_element_type=F32)
+        found = found.reshape(stencil, 2, 2 * SUB, cells)
+        found = found[:, 0] + found[:, 1]
+        for who in range(ns):
+            sums[q, who] = found[:, :, who * share : (who + 1) * share]
+        for off in range(ns - 1, 0, -1):
+            across(q, lax.rem(c + off, ns)).start()
+        keep(q).start()
+        return carry
+
+    lax.fori_loop(0, chunks, chunk, 0)
+
+    who = z // fold
     for j in range(stencil):
-        order[:, j, :] = total[j].T
-    out_ref[...] = order[...].reshape(cells * stencil, rows).T
-
-    def drain(dist, carry):
-        for q in range(len(cuts)):
+        rows = jnp.concatenate(
+            [sums[q, who, j, p * SUB : (p + 1) * SUB] for p in (0, 1) for q in range(chunks)]
+        )
+        lanes = jnp.concatenate([rows] * (LANES // (2 * shots))).T
+        order_own[pl.ds(j, share, stride=stencil), :] = lanes
+    outs = groups * stencil
+    mine = order_own[pl.ds(pl.multiple_of((z - who * fold) * outs, outs), outs), :]
+    b_ref[...] = mine.T[: 2 * shots].reshape(2, shots, outs)
+
+    def settle(q, carry):
+        keep(q).wait()
+        for off in range(1, ns):
+            peer = lax.rem(c + off, ns)
+            remote(
+                got.at[q, peer], got.at[q, peer], ss.at[q, peer], rs.at[q, peer], {"src": peer}
+            ).wait_recv()
+        return carry
+
+    lax.fori_loop(0, chunks, settle, 0)
+    for j in range(stencil):
+        rows = jnp.concatenate(
+            [
+                got[q, peer, j, p * SUB : (p + 1) * SUB]
+                for p in (0, 1)
+                for peer in range(ns)
+                for q in range(chunks)
+            ]
+        )
+        for g in range(2 * half // LANES):
+            order[g, pl.ds(j, share, stride=stencil), :] = rows[g * LANES : (g + 1) * LANES].T
+    for g in range(2 * half // LANES):
+        part, row = divmod(g * LANES, half)
+        p_ref[part, row : row + LANES, :] = order[g].T
+
+    def drain(q, carry):
+        def each(dist, inner):
             for lane in (0, 1):
                 block = z - dist * (1 - 2 * lane)
 
@@ -148,93 +249,61 @@
                 def _():
                     along(False, block, lane, dist, q).wait_send()
 
-        return carry
-
-    lax.fori_loop(0, nz, drain, 0)
-
-
-def bin_all(value, moveout, nz, groups, shots, cid):
+                    @pl.when(q == 0)
+                    def _():
+                        code(block, lane, dist).wait_send()
+
+            return inner
+
+        for off in range(1, ns):
+            across(q, lax.rem(c + off, ns)).wait_send()
+        return lax.fori_loop(0, nz, each, carry)
+
+    lax.fori_loop(0, chunks, drain, 0)
+
+
+def bin_all(traces, moveout, owner, group, table, nz, ns, bins, cid):
     tables, stencil = moveout.shape[1:]
-    width = value.shape[-1]
+    shots, _, width = traces.shape
+    groups = bins // stencil
+    fold = nz // ns
+    chunks = shots // SUB
+    share = nz * groups // ns
     weights = jnp.transpose(moveout, (0, 2, 1)).reshape(2 * stencil, tables)
-    cuts = pieces(value.shape, 3)
     dma = pltpu.SemaphoreType.DMA
     vmem = pl.BlockSpec(memory_space=pltpu.VMEM)
-    out = pl.pallas_call(
-        functools.partial(bin_kernel, nz, cuts, groups, tables, shots),
-        out_shape=jax.ShapeDtypeStruct((2 * shots, nz * groups * stencil), F32),
-        in_specs=[vmem, vmem],
-        out_specs=vmem,
+    part = (chunks, ns, stencil, 2 * SUB, share)
+    return pl.pallas_call(
+        functools.partial(bin_kernel, nz, ns, groups, tables, fold),
+        out_shape=(
+            jax.ShapeDtypeStruct((2, ns * shots, share * stencil), F32),
+            jax.ShapeDtypeStruct((2, shots, bins), F32),
+        ),
+        in_specs=[vmem] * 5,
+        out_specs=(vmem, vmem),
         scratch_shapes=[
-            pltpu.VMEM((nz,) + value.shape, F32),
-            pltpu.VMEM((stencil * 4 * shots, width), BF16),
-            pltpu.VMEM((stencil, 2 * shots, nz * groups), F32),
-            pltpu.VMEM((nz * groups, stencil, 2 * shots), F32),
-            dma((2, nz, len(cuts))),
-            dma((2, nz, len(cuts))),
+            pltpu.VMEM((nz, 3, width), jnp.int32),
+            pltpu.VMEM((nz, shots, 2, width), F32),
+            pltpu.VMEM((nz * groups, nz * width), BF16),
+            pltpu.VMEM((2 * stencil, nz * width), F32),
+            pltpu.VMEM((stencil * 4 * SUB, nz * width), BF16),
+            pltpu.VMEM(part, F32),
+            pltpu.VMEM(part, F32),
+            pltpu.VMEM((2 * ns * shots // LANES, share * stencil, LANES), F32),
+            pltpu.VMEM((share * stencil, LANES), F32),
+            dma((2, nz)),
+            dma((2, nz)),
+            dma((2, nz, chunks)),
+            dma((2, nz, chunks)),
+            dma((chunks, ns)),
+            dma((chunks, ns)),
+            dma((chunks,)),
         ],
         name="bin_all",
         compiler_params=pltpu.CompilerParams(
-            collective_id=cid, has_side_effects=True, vmem_limit_bytes=56 << 20
+            collective_id=cid, has_side_effects=True, vmem_limit_bytes=62 << 20
         ),
-    )(value, weights)
-    return out.reshape(2, shots, nz * groups * stencil)
-
-
-def spread_kernel(ns, in_ref, out_ref, ss, rs, ls):
-    c = lax.axis_index("src")
-    rows = in_ref.shape[1]
-    width = out_ref.shape[2]
-    barrier = pltpu.get_barrier_semaphore()
-    for off in range(1, ns):
-        pl.semaphore_signal(
-            barrier, inc=1, device_id={"src": lax.rem(c + off, ns)}, device_id_type=MESH
-        )
-    pl.semaphore_wait(barrier, ns - 1)
-
-    def part(who, p):
-        return in_ref.at[p, :, pl.ds(pl.multiple_of(who * width, 128), width)]
-
-    def place(who, p):
-        return out_ref.at[p, pl.ds(pl.multiple_of(who * rows, 8), rows), :]
-
-    sends = []
-    for off in range(1, ns):
-        for p in (0, 1):
-            who = lax.rem(c + off, ns)
-            copy = remote(
-                part(who, p), place(c, p), ss.at[off - 1, p], rs.at[off - 1, p], {"src": who}
-            )
-            copy.start()
-            sends.append(copy)
-    own = [pltpu.make_async_copy(part(c, p), place(c, p), ls.at[p]) for p in (0, 1)]
-    for copy in own:
-        copy.start()
-    for copy in own:
-        copy.wait()
-    for off in range(1, ns):
-        for p in (0, 1):
-            who = lax.rem(c + ns - off, ns)
-            remote(
-                place(who, p), place(who, p), ss.at[off - 1, p], rs.at[off - 1, p], {"src": who}
-            ).wait_recv()
-    for copy in sends:
-        copy.wait_send()
-
-
-def spread(value, ns, cid):
-    _, rows, width = value.shape
-    dma = pltpu.SemaphoreType.DMA
-    vmem = pl.BlockSpec(memory_space=pltpu.VMEM)
-    return pl.pallas_call(
-        functools.partial(spread_kernel, ns),
-        out_shape=jax.ShapeDtypeStruct((2, ns * rows, width // ns), F32),
-        in_specs=[vmem],
-        out_specs=vmem,
-        scratch_shapes=[dma((ns - 1, 2)), dma((ns - 1, 2)), dma((2,))],
-        name="spread",
-        compiler_params=pltpu.CompilerParams(collective_id=cid, has_side_effects=True),
-    )(value)
+    )(traces, owner[None], group[None], table[None], weights)
 
 
 def sweeps_kernel(
@@ -251,7 +320,11 @@
     half = ns * shots
     outs = steps * tile
     early = steps // 2
-    last = steps + 1
+    lag = LAG
+    hop = HOP
+    last = steps + lag - 1
+    soon = SOON
+    behind = BEHIND
 
     def a_copy(t):
         rows = pl.ds(pl.multiple_of(t * tile, tile), tile)
@@ -380,19 +453,23 @@
         def _():
             local(src, block, t).start()
 
-    def relay(t, dist):
+    def relay(t, dist, fresh, give_it):
         for lane in (0, 1):
             block = z - dist * (1 - 2 * lane)
 
             @pl.when((block >= 0) & (block < nz))
             def _():
-                along(held.at[block, t], block, lane, dist - 1, t).wait_recv()
-
-                @pl.when(has(lane))
-                def _():
-                    along(held.at[block, t], block, lane, dist, t).start()
-
-                hand_on(held.at[block, t], block, t)
+                @pl.when(jnp.asarray(fresh))
+                def _():
+                    along(held.at[block, t], block, lane, dist - 1, t).wait_recv()
+
+                    @pl.when(has(lane))
+                    def _():
+                        along(held.at[block, t], block, lane, dist, t).start()
+
+                @pl.when(jnp.asarray(give_it))
+                def _():
+                    hand_on(held.at[block, t], block, t)
 
     def first(step, carry):
         @pl.when(step < steps)
@@ -409,9 +486,9 @@
         def _():
             reduce_pair(0, step - 1)
 
-        @pl.when(step >= 2)
-        def _():
-            t = step - 2
+        @pl.when(step >= lag)
+        def _():
+            t = step - lag
             real, imag = finish(0, t)
             own[t, 0] = real
             own[t, 1] = imag
@@ -421,14 +498,16 @@
                 def _():
                     along(own.at[t], z, lane, 0, t).start()
 
-            hand_on(own.at[t], z, t)
+            @pl.when(t < soon)
+            def _():
+                hand_on(own.at[t], z, t)
 
         def earlier(dist, inner):
-            t = step - 2 - 2 * dist
+            t = step - lag - hop * dist
 
             @pl.when(t >= 0)
             def _():
-                relay(t, dist)
+                relay(t, dist, True, t < soon)
 
             return inner
 
@@ -437,11 +516,13 @@
     lax.fori_loop(0, last + 1, first, 0)
 
     def rest_of(t):
+        @pl.when(t >= soon)
+        def _():
+            hand_on(own.at[t], z, t)
+
         def each(dist, carry):
-            @pl.when(t + 2 + 2 * dist > last)
-            def _():
-                relay(t, dist)
-
+            fresh = t + lag + hop * dist > last
+            relay(t, dist, fresh, fresh | (t >= soon))
             return carry
 
         lax.fori_loop(1, nz, each, 0)
@@ -502,9 +583,9 @@
         def _():
             reduce_pair(1, step - 1)
 
-        @pl.when(step >= 2)
-        def _():
-            t = step - 2
+        @pl.when(step >= behind)
+        def _():
+            t = step - behind
             real, imag = finish(1, t)
             at = pl.ds(pl.multiple_of(t * tile, tile), tile)
             out_ref[0, :, at] = real
@@ -512,7 +593,7 @@
 
         return carry
 
-    lax.fori_loop(0, last + 1, second, 0)
+    lax.fori_loop(0, steps + behind, second, 0)
 
     def drain(t, carry):
         for sweep in (0, 1):
@@ -587,17 +668,9 @@
 
 
 def per_device(nz, ns, traces, moveout, owner, group, table, aperture, shaping):
-    groups = aperture.shape[1] // moveout.shape[2]
-    shots = traces.shape[0]
-    width = traces.shape[2]
-    codes = jnp.stack([owner, group, table]).astype(F32)
-    codes = jnp.concatenate([codes, jnp.zeros((5, width), F32)])
-    flat = jnp.transpose(traces, (1, 0, 2)).reshape(2 * shots, width)
-    everyone = bin_all(jnp.concatenate([flat, codes])[None], moveout, nz, groups, shots, 0)
     bins = aperture.shape[1]
-    binned = lax.dynamic_slice_in_dim(everyone, lax.axis_index("rcv") * bins, bins, 2)
+    columns, binned = bin_all(traces, moveout, owner, group, table, nz, ns, bins, 0)
     form = jnp.transpose(shaping, (1, 0, 2))
-    columns = spread(everyone, ns, 3)
     panel = two_sweeps(columns, binned, form, aperture, nz, ns, 2)
     return jnp.transpose(panel, (1, 0, 2))
 

time: 151 us -> 129 us (0.85)
  Pallas kernels: 143 us -> 124 us
  local copies, waits for them, and re-layouts: 6.34 us -> 4.38 us
  other arithmetic: 1.54 us -> 0 us
    pallas_call x1, Pallas kernels: 82 us -> 72.6 us  [two_sweeps(): pl.pallas_call(functools.partial(sweeps_kernel, nz, ns, shots, tile, step...]
    pallas_call x2 -> x1, Pallas kernels: 60.6 us -> 51.3 us  [bin_all(): pl.pallas_call(functools.partial(bin_kernel, nz, ns, groups, tables, fold...]
    dynamic_slice x1 -> x0, local copies, waits for them, and re-layouts: 1.88 us -> none  [per_device(): lax.dynamic_slice_in_dim(everyone, lax.axis_index('rcv') * bins, bins, 2)]
where the time goes in v2:
time: 129 us; the launch traced here: 128 us
  Pallas kernels  124 us (96%)
  local copies, waits for them, and re-layouts  4.38 us (3%)
    pallas_call x1, Pallas kernels, two_sweeps(): pl.pallas_call(functools.partial(sweeps_kernel, nz, ns, shots, tile, step...  72.6 us
    pallas_call x1, Pallas kernels, bin_all(): pl.pallas_call(functools.partial(bin_kernel, nz, ns, groups, tables, fold...  51.3 us

profile of v2, /device:TPU:0, one launch (start us, length us, event | category | flops | bytes accessed | tf_op | source)
XLA Modules:
  0.0 128.3 jit_solution(11700584787800264551)
XLA Ops:
  0.0 2.1 %copy.11 = f32[32,2,2048]{2,0,1:T(8,128)} copy(f32[32,2,2048]{2,1,0:T(2,128)} %param.13) | data formatting | bytes 1048576 | tf_op args[6]
  2.1 51.3 %bin_all.1 = (f32[2,128,2048]{2,1,0:T(8,128)}, f32[2,32,2048]{2,1,0:T(8,128)}) custom-call(f32[32,2,1024]{2,1,0:T(2,128)} %tr_ref.1, s32[1,1024]{1,0:T(1,128)} %bitcast.13, s32[1,1024]{1,0:T(1,128)} %bitcast.14, s32[1,1024]{1,0:T(1,128)} %bitcast.15, f32[32,32]{1,0:T(8,128)} %bitcast.12), custom_call_target="tpu_custom_call" | custom-call | tf_op jit(solution)/shard_map/bin_all/pallas_call | solution.py:276
  53.4 72.6 %two_sweeps.1 = f32[2,32,2048]{2,1,0:T(8,128)} custom-call(f32[2,128,2048]{2,1,0:T(8,128)} %get-tuple-element.7.p_ref, f32[2,32,2048]{2,1,0:T(8,128)} %get-tuple-element.8.b_ref, f32[2,32,2048]{2,1,0:T(8,128)} %bitcast.10, f32[2,2048,2048]{2,1,0:T(8,128)} %a_ref.1), custom_call_target="tpu_custom_call" | custom-call | tf_op jit(solution)/shard_map/two_sweeps/pallas_call | solution.py:634
  126.0 2.2 %copy.9 = f32[32,2,2048]{2,1,0:T(2,128)} copy(f32[32,2,2048]{2,0,1:T(8,128)} %bitcast.11) | data formatting | bytes 1048576 | tf_op jit(solution)/shard_map/transpose | solution.py:675

commit v3 on v2

v3 whole, which is shorter than its diff:
```python
import functools

import jax
import jax.numpy as jnp
from jax import lax
from jax.experimental import pallas as pl
from jax.experimental.pallas import tpu as pltpu
from jax.sharding import PartitionSpec as P

ITERS = 2
SUB = 8
LANES = 128
SOON = 4
LAG = 3
HOP = 1
BEHIND = 4
MESH = pl.DeviceIdType.MESH
F32 = jnp.float32
BF16 = jnp.bfloat16
NT = (((1,), (1,)), ((), ()))


def split(value):
    high = value.astype(BF16)
    return high, (value - high.astype(F32)).astype(BF16)


def remote(src, dst, send_sem, recv_sem, where):
    return pltpu.make_async_remote_copy(
        src_ref=src,
        dst_ref=dst,
        send_sem=send_sem,
        recv_sem=recv_sem,
        device_id=where,
        device_id_type=MESH,
    )


def kernel(
    nz, ns, groups, tables, fold, tile, steps,
    tr_ref, ow_ref, gr_ref, tb_ref, wt_ref, f_ref, a_ref, out_ref,
    codes, near, hot, picked, terms, found, sums, bins, order, b_own,
    a_all, high, low, mine, give, take, pass_on, got, own, held, cols, acc,
    cs, cr, ts, tr, xs, xr, xl,
    a_sem, s1, r1, s2, r2, zs, zr, ps, pr, ls,
):
    z = lax.axis_index("rcv")
    c = lax.axis_index("src")
    core = lax.rem(c, 2)
    chip = c // 2
    chips = ns // 2
    shots, _, width = tr_ref.shape
    stencil = wt_ref.shape[0] // 2
    chunks = shots // SUB
    cells = nz * groups
    share = cells // ns
    half = ns * shots
    outs = steps * tile
    early = steps // 2
    lag = LAG
    hop = HOP
    soon = SOON
    behind = BEHIND
    last = steps + lag - 1

    def a_copy(t):
        rows = pl.ds(pl.multiple_of(t * tile, tile), tile)
        return pltpu.make_async_copy(a_ref.at[:, rows, :], a_all.at[:, rows, :], a_sem.at[t])

    for t in range(min(2, steps)):
        a_copy(t).start()

    def has(lane):
        other = z + 1 - 2 * lane
        return (other >= 0) & (other < nz)

    barrier = pltpu.get_barrier_semaphore()
    for lane in (0, 1):

        @pl.when(has(lane))
        def _():
            pl.semaphore_signal(
                barrier, inc=1, device_id={"rcv": z + 1 - 2 * lane}, device_id_type=MESH
            )

    for off in range(1, ns):
        pl.semaphore_signal(
            barrier, inc=1, device_id={"src": lax.rem(c + off, ns)}, device_id_type=MESH
        )
    codes[z, 0:1] = ow_ref[...]
    codes[z, 1:2] = gr_ref[...]
    codes[z, 2:3] = tb_ref[...]
    peers = jnp.where(z > 0, 1, 0) + jnp.where(z < nz - 1, 1, 0)
    pl.semaphore_wait(barrier, peers + ns - 1)

    def span(q):
        return pl.ds(pl.multiple_of(q * SUB, SUB), SUB)

    def raw(own, block, lane, dist, q):
        return remote(
            tr_ref.at[span(q)] if own else near.at[block, span(q)],
            near.at[block, span(q)],
            ts.at[lane, dist, q],
            tr.at[lane, dist, q],
            {"rcv": z + 1 - 2 * lane},
        )

    def code(block, lane, dist):
        return remote(
            codes.at[block],
            codes.at[block],
            cs.at[lane, dist],
            cr.at[lane, dist],
            {"rcv": z + 1 - 2 * lane},
        )

    w = wt_ref[...]
    w0 = w.astype(BF16)
    rest = w - w0.astype(F32)
    w1 = rest.astype(BF16)
    w2 = (rest - w1.astype(F32)).astype(BF16)
    table_ids = lax.broadcasted_iota(jnp.int32, (tables, width), 0)
    cell_ids = lax.broadcasted_iota(jnp.int32, (cells, width), 0)

    def prepare(block):
        cell = codes[block, 0:1] * groups + codes[block, 1:2]
        hot[block] = jnp.where(cell_ids == cell, 1.0, 0.0).astype(BF16)
        table_hot = jnp.where(table_ids == codes[block, 2:3], 1.0, 0.0).astype(BF16)
        picked[block] = sum(
            jnp.dot(part, table_hot, preferred_element_type=F32) for part in (w0, w1, w2)
        )

    def add_in(real, imag, block, start):
        for j in range(stencil):
            wr = picked[block, j : j + 1]
            wi = picked[block, stencil + j : stencil + j + 1]
            both = jnp.concatenate([real * wr - imag * wi, real * wi + imag * wr])
            top, rest = split(both)
            base = j * 4 * SUB
            terms[base : base + 2 * SUB, :] = top
            terms[base + 2 * SUB : base + 4 * SUB, :] = rest
        now = lax.dot_general(terms[...], hot[block], NT, preferred_element_type=F32)
        found[...] = now if start else found[...] + now

    def swap(q, who):
        return remote(sums.at[q, who], bins.at[q, c], xs.at[q, who], xr.at[q, c], {"src": who})

    def keep(q):
        return pltpu.make_async_copy(sums.at[q, c], bins.at[q, c], xl.at[q])

    def relay_in(q, dist):
        for lane in (0, 1):
            block = z - dist * (1 - 2 * lane)

            @pl.when((block >= 0) & (block < nz))
            def _():
                @pl.when(jnp.asarray(q == 0))
                def _():
                    code(block, lane, dist - 1).wait_recv()

                    @pl.when(has(lane))
                    def _():
                        code(block, lane, dist).start()

                raw(False, block, lane, dist - 1, q).wait_recv()

                @pl.when(has(lane))
                def _():
                    raw(False, block, lane, dist, q).start()

    def chunk(q, carry):
        @pl.when(q == 0)
        def _():
            for lane in (0, 1):

                @pl.when(has(lane))
                def _():
                    code(z, lane, 0).start()
                    raw(True, z, lane, 0, 0).start()

        @pl.when(q + 1 < chunks)
        def _():
            for lane in (0, 1):

                @pl.when(has(lane))
                def _():
                    raw(True, z, lane, 0, q + 1).start()

        @pl.when(q == 0)
        def _():
            prepare(z)

        add_in(tr_ref[span(q), 0, :], tr_ref[span(q), 1, :], z, True)

        def hop_in(dist, inner):
            @pl.when((q == 0) | (dist > 1))
            def _():
                relay_in(q, dist)

            @pl.when((dist == nz - 1) & (q + 1 < chunks))
            def _():
                relay_in(q + 1, 1)

            def add(lane, deeper):
                block = z - dist * (1 - 2 * lane)

                @pl.when((block >= 0) & (block < nz))
                def _():
                    @pl.when(q == 0)
                    def _():
                        prepare(block)

                    add_in(near[block, span(q), 0, :], near[block, span(q), 1, :], block, False)

                return deeper

            return lax.fori_loop(0, 2, add, inner)

        lax.fori_loop(1, nz, hop_in, 0)
        both = found[...].reshape(stencil, 2, 2 * SUB, cells)
        both = both[:, 0] + both[:, 1]
        for who in range(ns):
            sums[q, who] = both[:, :, who * share : (who + 1) * share]
        for off in range(ns - 1, 0, -1):
            swap(q, lax.rem(c + off, ns)).start()
        keep(q).start()
        return carry

    lax.fori_loop(0, chunks, chunk, 0)

    who = z // fold
    for j in range(stencil):
        rows = jnp.concatenate(
            [sums[q, who, j, p * SUB : (p + 1) * SUB] for p in (0, 1) for q in range(chunks)]
        )
        lanes = jnp.concatenate([rows] * (LANES // (2 * shots))).T
        order[0, pl.ds(j, share, stride=stencil), :] = lanes
    base = order[0, pl.ds(pl.multiple_of((z - who * fold) * outs, outs), outs), :]
    b_own[...] = base.T[: 2 * shots].reshape(2, shots, outs)

    def settle(q, carry):
        keep(q).wait()
        for off in range(1, ns):
            peer = lax.rem(c + off, ns)
            remote(
                bins.at[q, peer], bins.at[q, peer], xs.at[q, peer], xr.at[q, peer], {"src": peer}
            ).wait_recv()
        return carry

    lax.fori_loop(0, chunks, settle, 0)
    for j in range(stencil):
        rows = jnp.concatenate(
            [
                bins[q, peer, j, p * SUB : (p + 1) * SUB]
                for p in (0, 1)
                for peer in range(ns)
                for q in range(chunks)
            ]
        )
        for g in range(2 * half // LANES):
            order[g, pl.ds(j, share, stride=stencil), :] = rows[g * LANES : (g + 1) * LANES].T
    for g in range(2 * half // LANES):
        part, row = divmod(g * LANES, half)
        top, rest = split(order[g].T)
        high[part * half + row : part * half + row + LANES, :] = top
        low[part * half + row : part * half + row + LANES, :] = rest

    def to_partner(sweep, t):
        return remote(
            give.at[t],
            take.at[t],
            s1.at[sweep, t],
            r1.at[sweep, t],
            {"src": c + 1 - 2 * core},
        )

    def to_chip(sweep, t, off):
        who = 2 * lax.rem(chip + off, chips) + core
        return remote(
            pass_on.at[t, off - 1],
            got.at[t, off - 1],
            s2.at[sweep, t, off - 1],
            r2.at[sweep, t, off - 1],
            {"src": who},
        )

    def times(t, ranges):
        rows = pl.ds(pl.multiple_of(t * tile, tile), tile)
        sums = []
        for part in (0, 1):
            total = None
            for cut in ranges:
                top, rest = split(a_all[part, rows, cut])
                now = lax.dot_general(high[:, cut], top, NT, preferred_element_type=F32)
                now += lax.dot_general(low[:, cut], top, NT, preferred_element_type=F32)
                now += lax.dot_general(high[:, cut], rest, NT, preferred_element_type=F32)
                total = now if total is None else total + now
            sums.append(total)
        return sums[0][:half] - sums[1][half:], sums[1][:half] + sums[0][half:]

    def hand_out(sweep, t, both):
        for part in (0, 1):
            for who in range(ns):
                value = both[part][who * shots : (who + 1) * shots]

                @pl.when(core == who % 2)
                def _():
                    mine[t, who // 2, part] = value

                @pl.when(core != who % 2)
                def _():
                    give[t, who // 2, part] = value

        to_partner(sweep, t).start()

    def reduce_pair(sweep, t):
        to_partner(sweep, t).wait_recv()
        for off in range(1, chips):
            there = lax.rem(chip + off, chips)
            pass_on[t, off - 1] = mine[t, there] + take[t, there]
            to_chip(sweep, t, off).start()
        mine[t, chip] += take[t, chip]

    def finish(sweep, t):
        found = mine[t, chip]
        for off in range(1, chips):
            to_chip(sweep, t, off).wait_recv()
            found += got[t, off - 1]
        at = pl.ds(pl.multiple_of(t * tile, tile), tile)
        fr, fi = f_ref[:, 0, at], f_ref[:, 1, at]
        return (
            b_own[0, :, at] - (fr * found[0] - fi * found[1]),
            b_own[1, :, at] - (fr * found[1] + fi * found[0]),
        )

    def along(src, block, lane, dist, t):
        return remote(
            src,
            held.at[block, t],
            zs.at[lane, dist, t],
            zr.at[lane, dist, t],
            {"rcv": z + 1 - 2 * lane},
        )

    def across(src, block, t):
        f = block - (block // fold) * fold
        return remote(
            src, cols.at[f, t, c], ps.at[block, t], pr.at[c, f, t], {"src": block // fold}
        )

    def local(src, block, t):
        f = block - (block // fold) * fold
        return pltpu.make_async_copy(src, cols.at[f, t, c], ls.at[f, t])

    def hand_on(src, block, t):
        @pl.when(block // fold != c)
        def _():
            across(src, block, t).start()

        @pl.when(block // fold == c)
        def _():
            local(src, block, t).start()

    def relay(t, dist, fresh, give_it):
        for lane in (0, 1):
            block = z - dist * (1 - 2 * lane)

            @pl.when((block >= 0) & (block < nz))
            def _():
                @pl.when(jnp.asarray(fresh))
                def _():
                    along(held.at[block, t], block, lane, dist - 1, t).wait_recv()

                    @pl.when(has(lane))
                    def _():
                        along(held.at[block, t], block, lane, dist, t).start()

                @pl.when(jnp.asarray(give_it))
                def _():
                    hand_on(held.at[block, t], block, t)

    def first(step, carry):
        @pl.when(step < steps)
        def _():
            a_copy(step).wait()

            @pl.when(step + 2 < steps)
            def _():
                a_copy(step + 2).start()

            hand_out(0, step, times(step, [pl.ds(0, fold * outs)]))

        @pl.when((step >= 1) & (step <= steps))
        def _():
            reduce_pair(0, step - 1)

        @pl.when(step >= lag)
        def _():
            t = step - lag
            real, imag = finish(0, t)
            own[t, 0] = real
            own[t, 1] = imag
            for lane in (0, 1):

                @pl.when(has(lane))
                def _():
                    along(own.at[t], z, lane, 0, t).start()

            @pl.when(t < soon)
            def _():
                hand_on(own.at[t], z, t)

        def earlier(dist, inner):
            t = step - lag - hop * dist

            @pl.when(t >= 0)
            def _():
                relay(t, dist, True, t < soon)

            return inner

        return lax.fori_loop(1, nz, earlier, carry)

    lax.fori_loop(0, last + 1, first, 0)

    def rest_of(t):
        @pl.when(t >= soon)
        def _():
            hand_on(own.at[t], z, t)

        def each(dist, carry):
            fresh = t + lag + hop * dist > last
            relay(t, dist, fresh, fresh | (t >= soon))
            return carry

        lax.fori_loop(1, nz, each, 0)

    def take_in(t, carry):
        for f in range(fold):
            local(own.at[t], c * fold + f, t).wait()
            for off in range(1, ns):
                who = lax.rem(c + off, ns)
                remote(
                    cols.at[f, t, who],
                    cols.at[f, t, who],
                    ps.at[0, t],
                    pr.at[who, f, t],
                    {"src": who},
                ).wait_recv()
            at = pl.ds(pl.multiple_of(f * outs + t * tile, tile), tile)
            for part in (0, 1):
                top, rest = split(cols[f, t, :, part].reshape(half, tile))
                high[part * half : (part + 1) * half, at] = top
                low[part * half : (part + 1) * half, at] = rest
        return carry

    def range_of(start, size):
        return [pl.ds(f * outs + start * tile, size * tile) for f in range(fold)]

    for t in range(early):
        rest_of(t)
    lax.fori_loop(0, early, take_in, 0)
    share = -(-steps // (steps - early))

    def between(t, carry):
        rest_of(t)

        def some(i, inner):
            r = (t - early) * share + i

            @pl.when(r < steps)
            def _():
                real, imag = times(r, range_of(0, early))
                acc[r, 0] = real
                acc[r, 1] = imag

            return inner

        return lax.fori_loop(0, share, some, carry)

    lax.fori_loop(early, steps, between, 0)
    lax.fori_loop(early, steps, take_in, 0)

    def sent(t, carry):
        to_partner(0, t).wait_send()
        for off in range(1, chips):
            to_chip(0, t, off).wait_send()
        return carry

    lax.fori_loop(0, steps, sent, 0)

    def second(step, carry):
        @pl.when(step < steps)
        def _():
            real, imag = times(step, range_of(early, steps - early))
            hand_out(1, step, (real + acc[step, 0], imag + acc[step, 1]))

        @pl.when((step >= 1) & (step <= steps))
        def _():
            reduce_pair(1, step - 1)

        @pl.when(step >= behind)
        def _():
            t = step - behind
            real, imag = finish(1, t)
            at = pl.ds(pl.multiple_of(t * tile, tile), tile)
            out_ref[:, 0, at] = real
            out_ref[:, 1, at] = imag

        return carry

    lax.fori_loop(0, steps + behind, second, 0)

    def drain(t, carry):
        to_partner(1, t).wait_send()
        for off in range(1, chips):
            to_chip(1, t, off).wait_send()

        def each(dist, inner):
            for lane in (0, 1):
                block = z - dist * (1 - 2 * lane)

                @pl.when((block >= 0) & (block < nz) & has(lane))
                def _():
                    along(held.at[block, t], block, lane, dist, t).wait_send()

            @pl.when(dist // fold != c)
            def _():
                across(held.at[dist, t], dist, t).wait_send()

            return inner

        return lax.fori_loop(0, nz, each, carry)

    lax.fori_loop(0, steps, drain, 0)

    def drain_in(q, carry):
        def each(dist, inner):
            for lane in (0, 1):
                block = z - dist * (1 - 2 * lane)

                @pl.when((block >= 0) & (block < nz) & has(lane))
                def _():
                    raw(False, block, lane, dist, q).wait_send()

                    @pl.when(q == 0)
                    def _():
                        code(block, lane, dist).wait_send()

            return inner

        for off in range(1, ns):
            swap(q, lax.rem(c + off, ns)).wait_send()
        return lax.fori_loop(0, nz, each, carry)

    lax.fori_loop(0, chunks, drain_in, 0)


def predict(traces, moveout, owner, group, table, aperture, shaping, nz, ns):
    tables, stencil = moveout.shape[1:]
    shots, _, width = traces.shape
    _, outs, depth = aperture.shape
    groups = outs // stencil
    fold = nz // ns
    chunks = shots // SUB
    cells = nz * groups
    share = cells // ns
    half = ns * shots
    tile = min(outs, 256)
    steps = outs // tile
    chips = ns // 2
    weights = jnp.transpose(moveout, (0, 2, 1)).reshape(2 * stencil, tables)
    dma = pltpu.SemaphoreType.DMA
    vmem = pl.BlockSpec(memory_space=pltpu.VMEM)
    part = (chunks, ns, stencil, 2 * SUB, share)
    block = (2, shots, tile)
    return pl.pallas_call(
        functools.partial(kernel, nz, ns, groups, tables, fold, tile, steps),
        out_shape=jax.ShapeDtypeStruct((shots, 2, outs), F32),
        in_specs=[vmem] * 6 + [pl.BlockSpec(memory_space=pl.ANY)],
        out_specs=vmem,
        scratch_shapes=[
            pltpu.VMEM((nz, 3, width), jnp.int32),
            pltpu.VMEM((nz, shots, 2, width), F32),
            pltpu.VMEM((nz, cells, width), BF16),
            pltpu.VMEM((nz, 2 * stencil, width), F32),
            pltpu.VMEM((stencil * 4 * SUB, width), BF16),
            pltpu.VMEM((stencil * 4 * SUB, cells), F32),
            pltpu.VMEM(part, F32),
            pltpu.VMEM(part, F32),
            pltpu.VMEM((2 * half // LANES, share * stencil, LANES), F32),
            pltpu.VMEM((2, shots, outs), F32),
            pltpu.VMEM((2, outs, depth), F32),
            pltpu.VMEM((2 * half, depth), BF16),
            pltpu.VMEM((2 * half, depth), BF16),
            pltpu.VMEM((steps, chips) + block, F32),
            pltpu.VMEM((steps, chips) + block, F32),
            pltpu.VMEM((steps, chips) + block, F32),
            pltpu.VMEM((steps, chips - 1) + block, F32),
            pltpu.VMEM((steps, chips - 1) + block, F32),
            pltpu.VMEM((steps,) + block, F32),
            pltpu.VMEM((nz, steps) + block, F32),
            pltpu.VMEM((fold, steps, ns) + block, F32),
            pltpu.VMEM((steps, 2, half, tile), F32),
            dma((2, nz)),
            dma((2, nz)),
            dma((2, nz, chunks)),
            dma((2, nz, chunks)),
            dma((chunks, ns)),
            dma((chunks, ns)),
            dma((chunks,)),
            dma((steps,)),
            dma((ITERS, steps)),
            dma((ITERS, steps)),
            dma((ITERS, steps, chips - 1)),
            dma((ITERS, steps, chips - 1)),
            dma((2, nz, steps)),
            dma((2, nz, steps)),
            dma((nz, steps)),
            dma((ns, fold, steps)),
            dma((fold, steps)),
        ],
        name="predict",
        compiler_params=pltpu.CompilerParams(
            collective_id=0, has_side_effects=True, vmem_limit_bytes=67043328
        ),
    )(traces, owner[None], group[None], table[None], weights, shaping, aperture)


def per_device(nz, ns, traces, moveout, owner, group, table, aperture, shaping):
    return predict(traces, moveout, owner, group, table, aperture, shaping, nz, ns)


def solution(mesh):
    nz, ns = mesh.shape["rcv"], mesh.shape["src"]
    in_specs = (
        P(("freq", "src"), None, "rcv"),
        P(None, "freq", None),
        P(("freq", "rcv")),
        P(("freq", "rcv")),
        P(("freq", "rcv")),
        P(None, ("freq", "rcv"), "src"),
        P(("freq", "src"), None, "rcv"),
    )
    out_specs = P(("freq", "src"), None, "rcv")
    return jax.shard_map(
        functools.partial(per_device, nz, ns),
        mesh=mesh,
        in_specs=in_specs,
        out_specs=out_specs,
        check_vma=False,
    )
```

time: 129 us -> 115 us (0.89)
  Pallas kernels: 124 us -> 113 us
  local copies, waits for them, and re-layouts: 4.38 us -> 1.87 us
    pallas_call x2 -> x1, Pallas kernels: 124 us -> 113 us  [predict(): pl.pallas_call(functools.partial(kernel, nz, ns, groups, tables, fold, ti...]
    transpose x1 -> x0, local copies, waits for them, and re-layouts: 2.24 us -> none  [per_device(): return jnp.transpose(panel, (1, 0, 2))]
where the time goes in v3:
time: 115 us; the launch traced here: 114 us
  Pallas kernels  113 us (98%)
  local copies, waits for them, and re-layouts  1.87 us (2%)
    pallas_call x1, Pallas kernels, predict(): pl.pallas_call(functools.partial(kernel, nz, ns, groups, tables, fold, ti...  113 us

profile of v3, /device:TPU:0, one launch (start us, length us, event | category | flops | bytes accessed | tf_op | source)
XLA Modules:
  0.0 114.4 jit_solution(9704000417501687933)
XLA Ops:
  0.0 112.6 %predict.1 = f32[32,2,2048]{2,1,0:T(2,128)} custom-call(f32[32,2,1024]{2,1,0:T(2,128)} %tr_ref.1, s32[1,1024]{1,0:T(1,128)} %bitcast.7, s32[1,1024]{1,0:T(1,128)} %bitcast.8, s32[1,1024]{1,0:T(1,128)} %bitcast.9, f32[32,32]{1,0:T(8,128)} %bitcast.6, f32[32,2,2048]{2,1,0:T(2,128)} %f_ref.1, f32[2,2048,2048]{2,1,0:T(8,128)} %a_ref.1), custom_call_target="tpu_custom_call" | custom-call | tf_op jit(solution)/shard_map/predict/pallas_call | solution.py:577
  112.6 1.9 %copy.9 = f32[32,2,2048]{2,1,0:T(2,128)} copy(f32[32,2,2048]{2,1,0:T(2,128)} %predict.1) | data formatting | bytes 1048576

commit v4 on v3

--- a/solution.py
+++ b/solution.py
@@ -11,6 +11,7 @@
 SUB = 8
 LANES = 128
 SOON = 4
+SOONER = 4
 LAG = 3
 HOP = 1
 BEHIND = 4
@@ -40,7 +41,7 @@
     nz, ns, groups, tables, fold, tile, steps,
     tr_ref, ow_ref, gr_ref, tb_ref, wt_ref, f_ref, a_ref, out_ref,
     codes, near, hot, picked, terms, found, sums, bins, order, b_own,
-    a_all, high, low, mine, give, take, pass_on, got, own, held, cols, acc,
+    a_all, pair, mine, give, take, pass_on, got, own, held, cols, acc,
     cs, cr, ts, tr, xs, xr, xl,
     a_sem, s1, r1, s2, r2, zs, zr, ps, pr, ls,
 ):
@@ -54,7 +55,6 @@
     chunks = shots // SUB
     cells = nz * groups
     share = cells // ns
-    half = ns * shots
     outs = steps * tile
     early = steps // 2
     lag = LAG
@@ -62,6 +62,9 @@
     soon = SOON
     behind = BEHIND
     last = steps + lag - 1
+    hs = shots // 2
+    side = ns * hs
+    sooner = min(SOONER, steps)
 
     def a_copy(t):
         rows = pl.ds(pl.multiple_of(t * tile, tile), tile)
@@ -238,32 +241,39 @@
     base = order[0, pl.ds(pl.multiple_of((z - who * fold) * outs, outs), outs), :]
     b_own[...] = base.T[: 2 * shots].reshape(2, shots, outs)
 
-    def settle(q, carry):
-        keep(q).wait()
-        for off in range(1, ns):
-            peer = lax.rem(c + off, ns)
-            remote(
-                bins.at[q, peer], bins.at[q, peer], xs.at[q, peer], xr.at[q, peer], {"src": peer}
-            ).wait_recv()
-        return carry
-
-    lax.fori_loop(0, chunks, settle, 0)
-    for j in range(stencil):
-        rows = jnp.concatenate(
-            [
-                bins[q, peer, j, p * SUB : (p + 1) * SUB]
-                for p in (0, 1)
-                for peer in range(ns)
-                for q in range(chunks)
-            ]
-        )
-        for g in range(2 * half // LANES):
-            order[g, pl.ds(j, share, stride=stencil), :] = rows[g * LANES : (g + 1) * LANES].T
-    for g in range(2 * half // LANES):
-        part, row = divmod(g * LANES, half)
-        top, rest = split(order[g].T)
-        high[part * half + row : part * half + row + LANES, :] = top
-        low[part * half + row : part * half + row + LANES, :] = rest
+    def settle(h):
+        first = h * chunks // 2
+
+        def each(q, carry):
+            keep(q).wait()
+            for off in range(1, ns):
+                peer = lax.rem(c + off, ns)
+                remote(
+                    bins.at[q, peer],
+                    bins.at[q, peer],
+                    xs.at[q, peer],
+                    xr.at[q, peer],
+                    {"src": peer},
+                ).wait_recv()
+            return carry
+
+        lax.fori_loop(first, first + chunks // 2, each, 0)
+        for j in range(stencil):
+            rows = jnp.concatenate(
+                [
+                    bins[first + q, peer, j, p * SUB : (p + 1) * SUB]
+                    for p in (0, 1)
+                    for peer in range(ns)
+                    for q in range(chunks // 2)
+                ]
+            )
+            for g in range(2 * side // LANES):
+                order[g, pl.ds(j, share, stride=stencil), :] = rows[g * LANES : (g + 1) * LANES].T
+        for g in range(2 * side // LANES):
+            top, rest = split(order[g].T)
+            row = h * 2 * side + g * LANES
+            pair[0, row : row + LANES, :] = top
+            pair[1, row : row + LANES, :] = rest
 
     def to_partner(sweep, t):
         return remote(
@@ -284,6 +294,26 @@
             {"src": who},
         )
 
+    def join(sums, row):
+        return (
+            sums[0][row : row + side] - sums[1][row + side : row + 2 * side],
+            sums[1][row : row + side] + sums[0][row + side : row + 2 * side],
+        )
+
+    def times_half(h, t):
+        rows = pl.ds(pl.multiple_of(t * tile, tile), tile)
+        mine = pl.ds(pl.multiple_of(h * 2 * side, 2 * side), 2 * side)
+        sums = []
+        for part in (0, 1):
+            top, rest = split(a_all[part, rows, :])
+            now = lax.dot_general(
+                pair[:, mine, :].reshape(4 * side, -1), top, NT, preferred_element_type=F32
+            )
+            now = now[: 2 * side] + now[2 * side :]
+            now += lax.dot_general(pair[0, mine, :], rest, NT, preferred_element_type=F32)
+            sums.append(now)
+        return join(sums, 0)
+
     def times(t, ranges):
         rows = pl.ds(pl.multiple_of(t * tile, tile), tile)
         sums = []
@@ -291,27 +321,25 @@
             total = None
             for cut in ranges:
                 top, rest = split(a_all[part, rows, cut])
-                now = lax.dot_general(high[:, cut], top, NT, preferred_element_type=F32)
-                now += lax.dot_general(low[:, cut], top, NT, preferred_element_type=F32)
-                now += lax.dot_general(high[:, cut], rest, NT, preferred_element_type=F32)
+                now = lax.dot_general(pair[0, :, cut], top, NT, preferred_element_type=F32)
+                now += lax.dot_general(pair[1, :, cut], top, NT, preferred_element_type=F32)
+                now += lax.dot_general(pair[0, :, cut], rest, NT, preferred_element_type=F32)
                 total = now if total is None else total + now
             sums.append(total)
-        return sums[0][:half] - sums[1][half:], sums[1][:half] + sums[0][half:]
-
-    def hand_out(sweep, t, both):
+        return join(sums, 0), join(sums, 2 * side)
+
+    def fill(t, h, both):
         for part in (0, 1):
             for who in range(ns):
-                value = both[part][who * shots : (who + 1) * shots]
+                value = both[part][who * hs : (who + 1) * hs]
 
                 @pl.when(core == who % 2)
                 def _():
-                    mine[t, who // 2, part] = value
+                    mine[t, who // 2, part, h * hs : (h + 1) * hs] = value
 
                 @pl.when(core != who % 2)
                 def _():
-                    give[t, who // 2, part] = value
-
-        to_partner(sweep, t).start()
+                    give[t, who // 2, part, h * hs : (h + 1) * hs] = value
 
     def reduce_pair(sweep, t):
         to_partner(sweep, t).wait_recv()
@@ -382,13 +410,22 @@
     def first(step, carry):
         @pl.when(step < steps)
         def _():
-            a_copy(step).wait()
-
-            @pl.when(step + 2 < steps)
-            def _():
-                a_copy(step + 2).start()
-
-            hand_out(0, step, times(step, [pl.ds(0, fold * outs)]))
+            @pl.when(step < sooner)
+            def _():
+                fill(step, 1, times_half(1, step))
+
+            @pl.when(step >= sooner)
+            def _():
+                a_copy(step).wait()
+
+                @pl.when(step + 2 < steps)
+                def _():
+                    a_copy(step + 2).start()
+
+                for h, both in enumerate(times(step, [pl.ds(0, fold * outs)])):
+                    fill(step, h, both)
+
+            to_partner(0, step).start()
 
         @pl.when((step >= 1) & (step <= steps))
         def _():
@@ -421,6 +458,19 @@
 
         return lax.fori_loop(1, nz, earlier, carry)
 
+    def before(t, carry):
+        a_copy(t).wait()
+
+        @pl.when(t + 2 < steps)
+        def _():
+            a_copy(t + 2).start()
+
+        fill(t, 0, times_half(0, t))
+        return carry
+
+    settle(0)
+    lax.fori_loop(0, sooner, before, 0)
+    settle(1)
     lax.fori_loop(0, last + 1, first, 0)
 
     def rest_of(t):
@@ -448,10 +498,13 @@
                     {"src": who},
                 ).wait_recv()
             at = pl.ds(pl.multiple_of(f * outs + t * tile, tile), tile)
-            for part in (0, 1):
-                top, rest = split(cols[f, t, :, part].reshape(half, tile))
-                high[part * half : (part + 1) * half, at] = top
-                low[part * half : (part + 1) * half, at] = rest
+            for h in (0, 1):
+                for part in (0, 1):
+                    value = cols[f, t, :, part, h * hs : (h + 1) * hs]
+                    top, rest = split(value.reshape(side, tile))
+                    row = (2 * h + part) * side
+                    pair[0, row : row + side, at] = top
+                    pair[1, row : row + side, at] = rest
         return carry
 
     def range_of(start, size):
@@ -470,9 +523,9 @@
 
             @pl.when(r < steps)
             def _():
-                real, imag = times(r, range_of(0, early))
-                acc[r, 0] = real
-                acc[r, 1] = imag
+                for h, both in enumerate(times(r, range_of(0, early))):
+                    acc[r, h, 0] = both[0]
+                    acc[r, h, 1] = both[1]
 
             return inner
 
@@ -492,8 +545,9 @@
     def second(step, carry):
         @pl.when(step < steps)
         def _():
-            real, imag = times(step, range_of(early, steps - early))
-            hand_out(1, step, (real + acc[step, 0], imag + acc[step, 1]))
+            for h, both in enumerate(times(step, range_of(early, steps - early))):
+                fill(step, h, (both[0] + acc[step, h, 0], both[1] + acc[step, h, 1]))
+            to_partner(1, step).start()
 
         @pl.when((step >= 1) & (step <= steps))
         def _():
@@ -588,11 +642,10 @@
             pltpu.VMEM((stencil * 4 * SUB, cells), F32),
             pltpu.VMEM(part, F32),
             pltpu.VMEM(part, F32),
-            pltpu.VMEM((2 * half // LANES, share * stencil, LANES), F32),
+            pltpu.VMEM((half // LANES, share * stencil, LANES), F32),
             pltpu.VMEM((2, shots, outs), F32),
             pltpu.VMEM((2, outs, depth), F32),
-            pltpu.VMEM((2 * half, depth), BF16),
-            pltpu.VMEM((2 * half, depth), BF16),
+            pltpu.VMEM((2, 2 * half, depth), BF16),
             pltpu.VMEM((steps, chips) + block, F32),
             pltpu.VMEM((steps, chips) + block, F32),
             pltpu.VMEM((steps, chips) + block, F32),
@@ -601,7 +654,7 @@
             pltpu.VMEM((steps,) + block, F32),
             pltpu.VMEM((nz, steps) + block, F32),
             pltpu.VMEM((fold, steps, ns) + block, F32),
-            pltpu.VMEM((steps, 2, half, tile), F32),
+            pltpu.VMEM((steps, 2, 2, half // 2, tile), F32),
             dma((2, nz)),
             dma((2, nz)),
             dma((2, nz, chunks)),

time: 115 us -> 113 us (0.983)
  Pallas kernels: 113 us -> 111 us
    pallas_call x1, Pallas kernels: 113 us -> 111 us  [predict(): pl.pallas_call(functools.partial(kernel, nz, ns, groups, tables, fold, ti...]
where the time goes in v4:
time: 113 us
  Pallas kernels  111 us (98%)
  local copies, waits for them, and re-layouts  1.87 us (2%)
    pallas_call x1, Pallas kernels, predict(): pl.pallas_call(functools.partial(kernel, nz, ns, groups, tables, fold, ti...  111 us

profile of v4, /device:TPU:0, one launch (start us, length us, event | category | flops | bytes accessed | tf_op | source)
XLA Modules:
  0.0 112.9 jit_solution(7436208046258863179)
XLA Ops:
  0.0 111.0 %predict.1 = f32[32,2,2048]{2,1,0:T(2,128)} custom-call(f32[32,2,1024]{2,1,0:T(2,128)} %tr_ref.1, s32[1,1024]{1,0:T(1,128)} %bitcast.7, s32[1,1024]{1,0:T(1,128)} %bitcast.8, s32[1,1024]{1,0:T(1,128)} %bitcast.9, f32[32,32]{1,0:T(8,128)} %bitcast.6, f32[32,2,2048]{2,1,0:T(2,128)} %f_ref.1, f32[2,2048,2048]{2,1,0:T(8,128)} %a_ref.1), custom_call_target="tpu_custom_call" | custom-call | tf_op jit(solution)/shard_map/predict/pallas_call | solution.py:631
  111.0 1.9 %copy.9 = f32[32,2,2048]{2,1,0:T(2,128)} copy(f32[32,2,2048]{2,1,0:T(2,128)} %predict.1) | data formatting | bytes 1048576

commit v5 on v4

--- a/solution.py
+++ b/solution.py
@@ -165,6 +165,8 @@
                     def _():
                         code(block, lane, dist).start()
 
+                    prepare(block)
+
                 raw(False, block, lane, dist - 1, q).wait_recv()
 
                 @pl.when(has(lane))
@@ -209,10 +211,6 @@
 
                 @pl.when((block >= 0) & (block < nz))
                 def _():
-                    @pl.when(q == 0)
-                    def _():
-                        prepare(block)
-
                     add_in(near[block, span(q), 0, :], near[block, span(q), 1, :], block, False)
 
                 return deeper

time: 113 us -> 112 us (level)
  no operation moved by 1% of the time
where the time goes in v5:
time: 112 us
  Pallas kernels  110 us (98%)
  local copies, waits for them, and re-layouts  1.87 us (2%)
    pallas_call x1, Pallas kernels, predict(): pl.pallas_call(functools.partial(kernel, nz, ns, groups, tables, fold, ti...  110 us

profile of v5, /device:TPU:0, one launch (start us, length us, event | category | flops | bytes accessed | tf_op | source)
XLA Modules:
  0.0 112.0 jit_solution(6787247140220126066)
XLA Ops:
  0.0 110.1 %predict.1 = f32[32,2,2048]{2,1,0:T(2,128)} custom-call(f32[32,2,1024]{2,1,0:T(2,128)} %tr_ref.1, s32[1,1024]{1,0:T(1,128)} %bitcast.7, s32[1,1024]{1,0:T(1,128)} %bitcast.8, s32[1,1024]{1,0:T(1,128)} %bitcast.9, f32[32,32]{1,0:T(8,128)} %bitcast.6, f32[32,2,2048]{2,1,0:T(2,128)} %f_ref.1, f32[2,2048,2048]{2,1,0:T(8,128)} %a_ref.1), custom_call_target="tpu_custom_call" | custom-call | tf_op jit(solution)/shard_map/predict/pallas_call | solution.py:629
  110.1 1.9 %copy.9 = f32[32,2,2048]{2,1,0:T(2,128)} copy(f32[32,2,2048]{2,1,0:T(2,128)} %predict.1) | data formatting | bytes 1048576
